TPU v7x, 32 devices: a whole 2x2x4 slice. The times are simulated.
32 devices in a mesh: rep: 2 (over y), shard: 16 (over z, x, core).
Axes of the slice: x: 2, y: 2, z: 4, core: 2. Of those that a mesh axis runs over, the one named last changes fastest.
Arguments:
- images: bfloat16 [32, 14, 14, 512], P(('rep', 'shard')), may hold values from -6 to 6
- cotangent: bfloat16 [32, 14, 14, 512], P(('rep', 'shard')), may hold values from -6 to 6
- regions: int32 [32, 14, 14], P(('rep', 'shard')), may hold values from 0 to 8, as said below
- w_qkv: bfloat16 [2, 512, 1536], P(None, 'shard'), may hold values from -0.25 to 0.25
- w_proj: bfloat16 [2, 512, 512], P(None, 'shard'), may hold values from -0.75 to 0.75
- w_fc1: bfloat16 [2, 512, 2048], P(None, 'shard'), may hold values from -0.25 to 0.25
- w_fc2: bfloat16 [2, 2048, 512], P(None, 'shard'), may hold values from -0.125 to 0.125
- norm_gains: bfloat16 [2, 2, 512], P(None, None, 'shard'), may hold values from 0.5 to 1.5
- norm_shifts: bfloat16 [2, 2, 512], P(None, None, 'shard'), may hold values from -1.1953125 to 1.1953125
- branch_biases: bfloat16 [2, 4, 512], P(None, None, 'shard'), may hold values from -1.1953125 to 1.1953125
- fc1_bias: bfloat16 [2, 2048], P(None, 'shard'), may hold values from -1.1953125 to 1.1953125
- rel_table: bfloat16 [2, 169, 16], replicated, may hold values from -6 to 6
Outputs:
- images_out: bfloat16 [32, 14, 14, 512], P(('rep', 'shard'))
- images_grad: float32 [32, 14, 14, 512], P(('rep', 'shard'))
- grad_w_qkv: float32 [2, 512, 1536], P(None, 'shard')
- grad_w_proj: float32 [2, 512, 512], P(None, 'shard')
- grad_w_fc1: float32 [2, 512, 2048], P(None, 'shard')
- grad_w_fc2: float32 [2, 2048, 512], P(None, 'shard')
- grad_norm_gains: float32 [2, 2, 512], P(None, None, 'shard')
- grad_norm_shifts: float32 [2, 2, 512], P(None, None, 'shard')
- grad_branch_biases: float32 [2, 4, 512], P(None, None, 'shard')
- grad_fc1_bias: float32 [2, 2048], P(None, 'shard')
- grad_rel_table: float32 [2, 169, 16], replicated
Inputs may be any that keep to these rules, and one draw needn't show every extreme that they name: `regions`: in each image the ids are 3 * (row band) + (column band), the rows and the columns each cut into three bands of consecutive positions.
All inputs are finite; a program needn't handle non-finite values.
Results may differ from a plain program's by a relative error of at most 0.023.
Values may be sent and summed in bfloat16 or wider, within the bound.
A program may use at most 128 MiB of HBM per device.

v0:
```python
import jax
import jax.numpy as jnp
from jax import lax
from jax.sharding import PartitionSpec as P

SIDE = 14
WIN = 7
SHIFT = 3


eps = 1e-05
highest = lax.Precision.HIGHEST
inv_root_two = 0.7071067811865476
inv_root_two_pi = 0.3989422804014327


def layer_norm(values, norm_gain, norm_shift):
    row_mean = jnp.mean(values, axis=-1, keepdims=True)
    centred = values - row_mean
    row_var = jnp.mean(centred * centred, axis=-1, keepdims=True)
    return centred * lax.rsqrt(row_var + eps) * norm_gain + norm_shift


def times_transposed(left, right):
    return lax.dot_general(
        left, right, (((1,), (1,)), ((), ())), preferred_element_type=jnp.float32
    )


def transposed_times(left, right):
    return lax.dot_general(
        left, right, (((0,), (0,)), ((), ())), preferred_element_type=jnp.float32
    )


def gelu_slope(pre_act):
    return 0.5 * (1.0 + lax.erf(pre_act * inv_root_two)) + pre_act * inv_root_two_pi * jnp.exp(
        -0.5 * pre_act * pre_act
    )


def to_windows(grid_data):
    image_count = grid_data.shape[0]
    per_side = SIDE // WIN
    trailing = grid_data.shape[3:]
    blocks = grid_data.reshape((image_count, per_side, WIN, per_side, WIN) + trailing)
    blocks = jnp.swapaxes(blocks, 2, 3)
    return blocks.reshape((image_count * per_side * per_side, WIN * WIN) + trailing)


def from_windows(blocks, image_count):
    per_side = SIDE // WIN
    trailing = blocks.shape[2:]
    grid_data = blocks.reshape((image_count, per_side, per_side, WIN, WIN) + trailing)
    grid_data = jnp.swapaxes(grid_data, 2, 3)
    return grid_data.reshape((image_count, SIDE, SIDE) + trailing)


def onehot_table():
    cell_ids = jnp.arange(WIN * WIN)
    cell_row = cell_ids // WIN
    cell_col = cell_ids % WIN
    table_side = 2 * WIN - 1
    rel_index = (cell_row[:, None] - cell_row[None, :] + WIN - 1) * table_side + (
        cell_col[:, None] - cell_col[None, :] + WIN - 1
    )
    rel_index = rel_index.reshape(-1)
    return (rel_index[:, None] == jnp.arange(table_side * table_side)[None, :]).astype(jnp.float32)


def replica_total(stacked):
    return (
        lax.psum(stacked[0].astype(jnp.bfloat16), "rep").astype(jnp.float32),
        lax.psum(stacked[1].astype(jnp.bfloat16), "rep").astype(jnp.float32),
        lax.psum(stacked[2].astype(jnp.bfloat16), "rep").astype(jnp.float32),
        lax.psum(stacked[3].astype(jnp.bfloat16), "rep").astype(jnp.float32),
        lax.psum(stacked[4].astype(jnp.bfloat16), "rep").astype(jnp.float32),
        lax.psum(stacked[5].astype(jnp.bfloat16), "rep").astype(jnp.float32),
        lax.psum(stacked[6].astype(jnp.bfloat16), "rep").astype(jnp.float32),
        lax.psum(stacked[7].astype(jnp.bfloat16), "rep").astype(jnp.float32),
    )


def body(
    images,
    cotangent,
    regions,
    w_qkv,
    w_proj,
    w_fc1,
    w_fc2,
    norm_gains,
    norm_shifts,
    branch_biases,
    fc1_bias,
    rel_table,
):
    layer_count = w_qkv.shape[0]
    image_count = images.shape[0]
    model_width = w_proj.shape[2]
    head_count = rel_table.shape[2]
    head_dim = model_width // head_count
    query_scale = head_dim ** (-0.5)
    column_scale = jnp.concatenate(
        [
            jnp.full((model_width,), query_scale, jnp.float32),
            jnp.ones((2 * model_width,), jnp.float32),
        ]
    )
    onehot = onehot_table()
    region_win = to_windows(regions)
    region_mask = jnp.where(region_win[:, :, None] == region_win[:, None, :], 0.0, -100.0).astype(
        jnp.float32
    )
    window_count = region_win.shape[0]
    tokens = window_count * WIN * WIN

    def score_bias(layer_num):
        table_rows = jnp.dot(onehot, rel_table[layer_num].astype(jnp.float32), precision=highest)
        bias_full = table_rows.T.reshape(head_count, WIN * WIN, WIN * WIN)[None]
        if layer_num % 2 == 1:
            bias_full = bias_full + region_mask[:, None]
        return bias_full

    def heads_of(flat):
        return flat.reshape(window_count, WIN * WIN, head_count, head_dim)

    residual = images.astype(jnp.float32)
    saved_acts = []
    kept_weights = []
    for layer_num in range(layer_count):
        shifted = layer_num % 2 == 1
        attn_w = (
            lax.all_gather(w_qkv[layer_num], "shard", axis=0, tiled=True),
            lax.all_gather(w_proj[layer_num], "shard", axis=0, tiled=True),
            lax.all_gather(norm_gains[layer_num], "shard", axis=1, tiled=True),
            lax.all_gather(norm_shifts[layer_num], "shard", axis=1, tiled=True),
            lax.all_gather(branch_biases[layer_num], "shard", axis=1, tiled=True),
        )
        mlp_w = (
            lax.all_gather(w_fc1[layer_num], "shard", axis=0, tiled=True),
            lax.all_gather(w_fc2[layer_num], "shard", axis=0, tiled=True),
            lax.all_gather(fc1_bias[layer_num], "shard", axis=0, tiled=True),
        )
        kept_weights.append((attn_w, mlp_w))
        wqkv, wproj, gains, shifts, biases = attn_w
        gains = gains.astype(jnp.float32)
        shifts = shifts.astype(jnp.float32)
        biases = biases.astype(jnp.float32)
        normed = layer_norm(residual, gains[0], shifts[0]).astype(jnp.bfloat16)
        if shifted:
            normed = jnp.roll(normed, (-SHIFT, -SHIFT), axis=(1, 2))
        window_rows = to_windows(normed).reshape(tokens, model_width)
        projected = jnp.dot(window_rows, wqkv, preferred_element_type=jnp.float32)
        queries = heads_of(
            ((projected[:, :model_width] + biases[0]) * query_scale).astype(jnp.bfloat16)
        )
        key_rows = heads_of(projected[:, model_width : 2 * model_width].astype(jnp.bfloat16))
        values = heads_of((projected[:, 2 * model_width :] + biases[1]).astype(jnp.bfloat16))
        scores = jnp.einsum(
            "nqhd,nkhd->nhqk", queries, key_rows, preferred_element_type=jnp.float32
        ) + score_bias(layer_num)
        row_max = jnp.max(scores, axis=-1, keepdims=True)
        log_total = row_max + jnp.log(jnp.sum(jnp.exp(scores - row_max), axis=-1, keepdims=True))
        attn_probs = jnp.exp(scores - log_total).astype(jnp.bfloat16)
        mixed_rows = jnp.einsum(
            "nhqk,nkhd->nqhd", attn_probs, values, preferred_element_type=jnp.float32
        )
        mixed_rows = mixed_rows.reshape(tokens, model_width).astype(jnp.bfloat16)
        branch = jnp.dot(mixed_rows, wproj, preferred_element_type=jnp.float32) + biases[2]
        branch = from_windows(branch.reshape(window_count, WIN * WIN, model_width), image_count)
        if shifted:
            branch = jnp.roll(branch, (SHIFT, SHIFT), axis=(1, 2))
        middle = residual + branch
        wfirst, wsecond, bias_first = mlp_w
        normed_mlp = (
            layer_norm(middle, gains[1], shifts[1]).astype(jnp.bfloat16).reshape(-1, model_width)
        )
        pre_act = jnp.dot(
            normed_mlp, wfirst, preferred_element_type=jnp.float32
        ) + bias_first.astype(jnp.float32)
        activated = jax.nn.gelu(pre_act, approximate=False).astype(jnp.bfloat16)
        mlp_out = jnp.dot(activated, wsecond, preferred_element_type=jnp.float32) + biases[3]
        saved_acts.append(
            (
                residual,
                window_rows,
                queries,
                key_rows,
                values,
                log_total,
                mixed_rows,
                middle,
                normed_mlp,
                pre_act,
                activated,
            )
        )
        residual = middle + mlp_out.reshape(middle.shape)
    images_out = residual.astype(jnp.bfloat16)
    upstream = cotangent.astype(jnp.float32)
    layer_grads = [None] * layer_count
    table_list = [None] * layer_count
    for layer_num in reversed(range(layer_count)):
        shifted = layer_num % 2 == 1
        (
            residual_in,
            window_rows,
            queries,
            key_rows,
            values,
            log_total,
            mixed_rows,
            middle,
            normed_mlp,
            pre_act,
            activated,
        ) = saved_acts[layer_num]
        wqkv, wproj, gains, shifts, biases = (
            lax.all_gather(w_qkv[layer_num], "shard", axis=0, tiled=True),
            lax.all_gather(w_proj[layer_num], "shard", axis=0, tiled=True),
            lax.all_gather(norm_gains[layer_num], "shard", axis=1, tiled=True),
            lax.all_gather(norm_shifts[layer_num], "shard", axis=1, tiled=True),
            lax.all_gather(branch_biases[layer_num], "shard", axis=1, tiled=True),
        )
        wfirst, wsecond, bias_first = (
            lax.all_gather(w_fc1[layer_num], "shard", axis=0, tiled=True),
            lax.all_gather(w_fc2[layer_num], "shard", axis=0, tiled=True),
            lax.all_gather(fc1_bias[layer_num], "shard", axis=0, tiled=True),
        )
        gains = gains.astype(jnp.float32)
        shifts = shifts.astype(jnp.float32)
        out_grad = upstream.astype(jnp.bfloat16).reshape(-1, model_width)
        grad_b_second = jnp.sum(out_grad.astype(jnp.float32), axis=0)
        grad_w_second = transposed_times(activated, out_grad)
        act_grad = times_transposed(out_grad, wsecond)
        pre_grad = (act_grad * gelu_slope(pre_act)).astype(jnp.bfloat16)
        grad_b_first = jnp.sum(pre_grad.astype(jnp.float32), axis=0)
        grad_w_first = transposed_times(normed_mlp, pre_grad)
        norm_grad = times_transposed(pre_grad, wfirst).reshape(middle.shape)
        norm_pull = jax.vjp(layer_norm, middle, gains[1], shifts[1])[1]
        middle_part, grad_gain_mlp, grad_shift_mlp = norm_pull(norm_grad)
        middle_grad = upstream + middle_part
        branch_grad = middle_grad
        if shifted:
            branch_grad = jnp.roll(branch_grad, (-SHIFT, -SHIFT), axis=(1, 2))
        branch_rows = to_windows(branch_grad.astype(jnp.bfloat16)).reshape(tokens, model_width)
        grad_b_proj = jnp.sum(branch_rows.astype(jnp.float32), axis=0)
        grad_w_proj = transposed_times(mixed_rows, branch_rows)
        mixed_grad = heads_of(times_transposed(branch_rows, wproj).astype(jnp.bfloat16))
        scores = jnp.einsum(
            "nqhd,nkhd->nhqk", queries, key_rows, preferred_element_type=jnp.float32
        ) + score_bias(layer_num)
        attn_probs = jnp.exp(scores - log_total)
        prob_grad = jnp.einsum(
            "nqhd,nkhd->nhqk", mixed_grad, values, preferred_element_type=jnp.float32
        )
        value_grad = jnp.einsum(
            "nhqk,nqhd->nkhd",
            attn_probs.astype(jnp.bfloat16),
            mixed_grad,
            preferred_element_type=jnp.float32,
        ).astype(jnp.bfloat16)
        score_grad = (
            attn_probs * (prob_grad - jnp.sum(attn_probs * prob_grad, axis=-1, keepdims=True))
        ).astype(jnp.bfloat16)
        table_term = jnp.sum(score_grad.astype(jnp.float32), axis=0).reshape(head_count, -1).T
        table_list[layer_num] = jnp.dot(onehot.T, table_term, precision=highest)
        query_grad = jnp.einsum(
            "nhqk,nkhd->nqhd", score_grad, key_rows, preferred_element_type=jnp.float32
        ).astype(jnp.bfloat16)
        key_grad = jnp.einsum(
            "nhqk,nqhd->nkhd", score_grad, queries, preferred_element_type=jnp.float32
        ).astype(jnp.bfloat16)
        qkv_grad = jnp.concatenate(
            [
                query_grad.reshape(tokens, model_width),
                key_grad.reshape(tokens, model_width),
                value_grad.reshape(tokens, model_width),
            ],
            axis=1,
        )
        grad_w_proj_qkv = transposed_times(window_rows, qkv_grad) * column_scale[None, :]
        grad_b_query = (
            jnp.sum(query_grad.reshape(tokens, model_width).astype(jnp.float32), axis=0)
            * query_scale
        )
        grad_b_value = jnp.sum(value_grad.reshape(tokens, model_width).astype(jnp.float32), axis=0)
        rows_grad = times_transposed(qkv_grad[:, :model_width], wqkv[:, :model_width]) * query_scale
        rows_grad = rows_grad + times_transposed(qkv_grad[:, model_width:], wqkv[:, model_width:])
        normed_grad = from_windows(
            rows_grad.reshape(window_count, WIN * WIN, model_width), image_count
        )
        if shifted:
            normed_grad = jnp.roll(normed_grad, (SHIFT, SHIFT), axis=(1, 2))
        first_pull = jax.vjp(layer_norm, residual_in, gains[0], shifts[0])[1]
        input_part, grad_gain_attn, grad_shift_attn = first_pull(normed_grad)
        upstream = middle_grad + input_part
        gain_grads = jnp.stack([grad_gain_attn, grad_gain_mlp])
        shift_grads = jnp.stack([grad_shift_attn, grad_shift_mlp])
        bias_grads = jnp.stack([grad_b_query, grad_b_value, grad_b_proj, grad_b_second])
        qkv_share, proj_share, gain_share, shift_share, bias_share = (
            lax.psum_scatter(
                grad_w_proj_qkv.astype(jnp.bfloat16), "shard", scatter_dimension=0, tiled=True
            ).astype(jnp.float32),
            lax.psum_scatter(
                grad_w_proj.astype(jnp.bfloat16), "shard", scatter_dimension=0, tiled=True
            ).astype(jnp.float32),
            lax.psum_scatter(
                gain_grads.astype(jnp.bfloat16), "shard", scatter_dimension=1, tiled=True
            ).astype(jnp.float32),
            lax.psum_scatter(
                shift_grads.astype(jnp.bfloat16), "shard", scatter_dimension=1, tiled=True
            ).astype(jnp.float32),
            lax.psum_scatter(
                bias_grads.astype(jnp.bfloat16), "shard", scatter_dimension=1, tiled=True
            ).astype(jnp.float32),
        )
        first_share, second_share, bfirst_share = (
            lax.psum_scatter(
                grad_w_first.astype(jnp.bfloat16), "shard", scatter_dimension=0, tiled=True
            ).astype(jnp.float32),
            lax.psum_scatter(
                grad_w_second.astype(jnp.bfloat16), "shard", scatter_dimension=0, tiled=True
            ).astype(jnp.float32),
            lax.psum_scatter(
                grad_b_first.astype(jnp.bfloat16), "shard", scatter_dimension=0, tiled=True
            ).astype(jnp.float32),
        )
        layer_grads[layer_num] = (
            qkv_share,
            proj_share,
            first_share,
            second_share,
            gain_share,
            shift_share,
            bias_share,
            bfirst_share,
        )
    stacked = [jnp.stack([layer_grads[n][m] for n in range(layer_count)]) for m in range(8)]
    summed = replica_total(stacked)
    table_total = lax.psum(jnp.stack(table_list), ("rep", "shard"))
    return (
        images_out,
        upstream,
        summed[0],
        summed[1],
        summed[2],
        summed[3],
        summed[4],
        summed[5],
        summed[6],
        summed[7],
        table_total,
    )


def solution(mesh):
    return jax.shard_map(
        body,
        mesh=mesh,
        in_specs=(
            P(("rep", "shard"), None, None, None),
            P(("rep", "shard"), None, None, None),
            P(("rep", "shard"), None, None),
            P(None, "shard", None),
            P(None, "shard", None),
            P(None, "shard", None),
            P(None, "shard", None),
            P(None, None, "shard"),
            P(None, None, "shard"),
            P(None, None, "shard"),
            P(None, "shard"),
            P(),
        ),
        out_specs=(
            P(("rep", "shard"), None, None, None),
            P(("rep", "shard"), None, None, None),
            P(None, "shard", None),
            P(None, "shard", None),
            P(None, "shard", None),
            P(None, "shard", None),
            P(None, None, "shard"),
            P(None, None, "shard"),
            P(None, None, "shard"),
            P(None, "shard"),
            P(),
        ),
        check_vma=False,
    )
```

profile of v0, /device:TPU:0, one launch (start us, length us, event | category | flops | bytes accessed | tf_op | source)
XLA Modules:
  0.0 1341.8 jit_solution(16533433941194631323)
XLA Ops:
  17.5 24.0 %all-gather = bf16[1,2,512]{1,0,2:T(2,128)(2,1)S(1)} all-gather(bf16[1,2,32]{1,0,2:T(2,128)(2,1)S(1)} %copy.412), channel_id=2, replica_groups=mesh['rep'=2,'shard'=16] {'shard'}, dimensions={2}, use_global_device_ids=true | all-gather | bytes 2176 | tf_op jit(solution)/shard_map/all_gather | solution.py:136
  44.6 18.3 %all-gather.1 = bf16[1,2,512]{1,0,2:T(2,128)(2,1)S(1)} all-gather(bf16[1,2,32]{1,0,2:T(2,128)(2,1)S(1)} %copy.413), channel_id=3, replica_groups=mesh['rep'=2,'shard'=16] {'shard'}, dimensions={2}, use_global_device_ids=true | all-gather | bytes 2176 | tf_op jit(solution)/shard_map/all_gather | solution.py:137
  67.9 20.7 %all-gather.3 = bf16[1,4,512]{1,0,2:T(2,128)(2,1)S(1)} all-gather(bf16[1,4,32]{1,0,2:T(2,128)(2,1)S(1)} %copy.414), channel_id=5, replica_groups=mesh['rep'=2,'shard'=16] {'shard'}, dimensions={2}, use_global_device_ids=true | all-gather | bytes 4352 | tf_op jit(solution)/shard_map/all_gather | solution.py:138
  96.1 19.4 %all-gather.4 = bf16[1,512,512]{2,1,0:T(8,128)(2,1)S(1)} all-gather(bf16[1,32,512]{2,1,0:T(8,128)(2,1)S(1)} %get-tuple-element.155), channel_id=6, replica_groups=mesh['rep'=2,'shard'=16] {'shard'}, dimensions={1}, use_global_device_ids=true | all-gather | bytes 557056 | tf_op jit(solution)/shard_map/all_gather | solution.py:135
  115.5 18.6 %all-gather.6 = bf16[1,2048]{1,0:T(2,128)(2,1)S(1)} all-gather(bf16[1,128]{1,0:T(2,128)(2,1)S(1)} %get-tuple-element.163), channel_id=8, replica_groups=mesh['rep'=2,'shard'=16] {'shard'}, dimensions={1}, use_global_device_ids=true | all-gather | bytes 4352 | tf_op jit(solution)/shard_map/all_gather | solution.py:143
  134.3 18.2 %all-gather.8 = bf16[1,2,512]{1,0,2:T(2,128)(2,1)S(1)} all-gather(bf16[1,2,32]{1,0,2:T(2,128)(2,1)S(1)} %copy.415), channel_id=10, replica_groups=mesh['rep'=2,'shard'=16] {'shard'}, dimensions={2}, use_global_device_ids=true | all-gather | bytes 2176 | tf_op jit(solution)/shard_map/all_gather | solution.py:136
  156.2 19.6 %all-gather.9 = bf16[1,2,512]{1,0,2:T(2,128)(2,1)S(1)} all-gather(bf16[1,2,32]{1,0,2:T(2,128)(2,1)S(1)} %copy.416), channel_id=11, replica_groups=mesh['rep'=2,'shard'=16] {'shard'}, dimensions={2}, use_global_device_ids=true | all-gather | bytes 2176 | tf_op jit(solution)/shard_map/all_gather | solution.py:137
  179.4 31.4 %all-gather.11 = bf16[1,4,512]{1,0,2:T(2,128)(2,1)S(1)} all-gather(bf16[1,4,32]{1,0,2:T(2,128)(2,1)S(1)} %copy.417), channel_id=13, replica_groups=mesh['rep'=2,'shard'=16] {'shard'}, dimensions={2}, use_global_device_ids=true | all-gather | bytes 4352 | tf_op jit(solution)/shard_map/all_gather | solution.py:138
  220.6 21.8 %all-gather.12 = bf16[1,512,512]{2,1,0:T(8,128)(2,1)} all-gather(bf16[1,32,512]{2,1,0:T(8,128)(2,1)S(1)} %get-tuple-element.154), channel_id=14, replica_groups=mesh['rep'=2,'shard'=16] {'shard'}, dimensions={1}, use_global_device_ids=true | all-gather | bytes 557056 | tf_op jit(solution)/shard_map/all_gather | solution.py:135
  497.7 31.7 %all-reduce.2 = (bf16[2048]{0:T(1024)(128)(2,1)S(1)}, bf16[2048]{0:T(1024)(128)(2,1)S(1)}) all-reduce(bf16[2048]{0:T(1024)(128)(2,1)S(1)} %copy-done.107, bf16[2048]{0:T(1024)(128)(2,1)S(1)} %copy-done.108), channel_id=33, replica_groups=mesh['rep'=2,'shard'=16] {'shard'}, use_global_device_ids=true, to_apply=%region_63.64.clone | all-reduce | flops 4096 | bytes 16384
  534.4 37.7 %psum.71 = f32[2,169,16]{1,2,0:T(8,128)} all-reduce(f32[2,169,16]{1,2,0:T(8,128)S(1)} %pad_maximum_fusion.10), channel_id=1, replica_groups=mesh['rep'=2,'shard'=16] {'rep','shard'}, use_global_device_ids=true, to_apply=%region_67.68 | all-reduce | flops 5408 | bytes 43264 | tf_op jit(solution)/shard_map/psum | solution.py:342
  573.6 53.1 %reduce-scatter.27.cloned.1.call-done = bf16[32,1536]{1,0:T(8,128)(2,1)} async-done(((bf16[512,1536]{1,0:T(8,128)(2,1)}), bf16[32,1536]{1,0:T(8,128)(2,1)}) %reduce-scatter.27.cloned.1.call-update) | async-done | bytes 98320 | tf_op jit(solution)/shard_map/reduce_scatter | solution.py:303
  626.7 62.5 %reduce-scatter.29.cloned.1.call-done = bf16[32,1536]{1,0:T(8,128)(2,1)} async-done(((bf16[512,1536]{1,0:T(8,128)(2,1)}), bf16[32,1536]{1,0:T(8,128)(2,1)}) %reduce-scatter.29.cloned.1.call-update) | async-done | bytes 98320 | tf_op jit(solution)/shard_map/reduce_scatter | solution.py:303
  690.8 62.7 %reduce-scatter.37.cloned.1.call-done = bf16[32,2048]{1,0:T(8,128)(2,1)} async-done(((bf16[512,2048]{1,0:T(8,128)(2,1)}), bf16[32,2048]{1,0:T(8,128)(2,1)}) %reduce-scatter.37.cloned.1.call-update) | async-done | bytes 131088 | tf_op jit(solution)/shard_map/reduce_scatter | solution.py:320
  753.6 64.6 %reduce-scatter.35.cloned.1.call-done = bf16[32,2048]{1,0:T(8,128)(2,1)} async-done(((bf16[512,2048]{1,0:T(8,128)(2,1)}), bf16[32,2048]{1,0:T(8,128)(2,1)}) %reduce-scatter.35.cloned.1.call-update) | async-done | bytes 131088 | tf_op jit(solution)/shard_map/reduce_scatter | solution.py:320
  819.9 62.6 %reduce-scatter.39.cloned.1.call-done = bf16[128,512]{1,0:T(8,128)(2,1)} async-done(((bf16[2048,512]{1,0:T(8,128)(2,1)}), bf16[128,512]{1,0:T(8,128)(2,1)}) %reduce-scatter.39.cloned.1.call-update) | async-done | bytes 131088 | tf_op jit(solution)/shard_map/reduce_scatter | solution.py:323
  882.4 64.7 %reduce-scatter.41.cloned.1.call-done = bf16[128,512]{1,0:T(8,128)(2,1)} async-done(((bf16[2048,512]{1,0:T(8,128)(2,1)}), bf16[128,512]{1,0:T(8,128)(2,1)}) %reduce-scatter.41.cloned.1.call-update) | async-done | bytes 131088 | tf_op jit(solution)/shard_map/reduce_scatter | solution.py:323
  950.1 54.4 %reduce-scatter.47.cloned.1.call-done = bf16[32,2]{1,0:T(8,128)(2,1)} async-done(((bf16[512,2]{1,0:T(8,128)(2,1)}), bf16[32,2]{1,0:T(8,128)(2,1)}) %reduce-scatter.47.cloned.1.call-update) | async-done | bytes 144
  1005.3 56.7 %reduce-scatter.49.cloned.1.call-done = bf16[32,2]{1,0:T(8,128)(2,1)} async-done(((bf16[512,2]{1,0:T(8,128)(2,1)}), bf16[32,2]{1,0:T(8,128)(2,1)}) %reduce-scatter.49.cloned.1.call-update) | async-done | bytes 144
  1062.8 56.7 %reduce-scatter.43.cloned.1.call-done = bf16[32,2]{1,0:T(8,128)(2,1)} async-done(((bf16[512,2]{1,0:T(8,128)(2,1)}), bf16[32,2]{1,0:T(8,128)(2,1)}) %reduce-scatter.43.cloned.1.call-update) | async-done | bytes 144
  1120.2 57.2 %reduce-scatter.45.cloned.1.call-done = bf16[32,2]{1,0:T(8,128)(2,1)} async-done(((bf16[512,2]{1,0:T(8,128)(2,1)}), bf16[32,2]{1,0:T(8,128)(2,1)}) %reduce-scatter.45.cloned.1.call-update) | async-done | bytes 144
  1178.3 56.8 %reduce-scatter.51.cloned.1.call-done = bf16[32,4]{1,0:T(8,128)(2,1)} async-done(((bf16[512,4]{1,0:T(8,128)(2,1)}), bf16[32,4]{1,0:T(8,128)(2,1)}) %reduce-scatter.51.cloned.1.call-update) | async-done | bytes 272
  1235.8 56.7 %reduce-scatter.53.cloned.1.call-done = bf16[32,4]{1,0:T(8,128)(2,1)} async-done(((bf16[512,4]{1,0:T(8,128)(2,1)}), bf16[32,4]{1,0:T(8,128)(2,1)}) %reduce-scatter.53.cloned.1.call-update) | async-done | bytes 272
  1300.6 28.8 %all-reduce.7.cloned.1.call-done = (bf16[2,32,1536]{2,1,0:T(8,128)(2,1)}, bf16[2,32,512]{2,1,0:T(8,128)(2,1)}, bf16[2,32,2048]{2,1,0:T(8,128)(2,1)}, bf16[2,128,512]{2,1,0:T(8,128)(2,1)}) async-done(((bf16[2,32,1536]{2,1,0:T(8,128)(2,1)}, bf16[2,32,512]{2,1,0:T(8,128)(2,1)}, bf16[2,32,2048]{2,1,0:T(8,128)(2,1)}, bf16[2,128,512]{2,1,0:T(8,128)(2,1)}), (bf16[2,32,1536]{2,1,0:T(8,128)(2,1)}, ...) | async-done | bytes 786448 | tf_op jit(solution)/shard_map/psum | solution.py:73
  (556 shorter events, 325.5 us)
Async XLA Ops:
  7.2 253.9 %all-gather.23.cloned.1.call-start = ((), (), s32[]{:S(2)}) async-start(), calls=%async_computation.22 | async-start | bytes 1671168 | tf_op jit(solution)/shard_map/all_gather | solution.py:134
  8.9 275.0 %all-gather.25.cloned.1.call-start = ((), (), s32[]{:S(2)}) async-start(), calls=%async_computation.23 | async-start | bytes 2228224 | tf_op jit(solution)/shard_map/all_gather | solution.py:141
  10.7 280.6 %all-gather.27.cloned.1.call-start = ((), (), s32[]{:S(2)}) async-start(), calls=%async_computation.24 | async-start | bytes 2228224 | tf_op jit(solution)/shard_map/all_gather | solution.py:142
  12.4 288.5 %all-gather.29.cloned.1.call-start = ((), (), s32[]{:S(2)}) async-start(), calls=%async_computation.25 | async-start | bytes 1671168 | tf_op jit(solution)/shard_map/all_gather | solution.py:134
  13.0 321.2 %all-gather.31.cloned.1.call-start = ((), (), s32[]{:S(2)}) async-start(), calls=%async_computation.26 | async-start | bytes 2228224 | tf_op jit(solution)/shard_map/all_gather | solution.py:141
  13.6 327.7 %all-gather.33.cloned.1.call-start = ((), (), s32[]{:S(2)}) async-start(), calls=%async_computation.27 | async-start | bytes 2228224 | tf_op jit(solution)/shard_map/all_gather | solution.py:142
  14.2 558.0 %reduce-scatter.33.cloned.1.call-start = ((), (), s32[]{:S(2)}) async-start(), calls=%async_computation.17 | async-start | bytes 557056 | tf_op jit(solution)/shard_map/reduce_scatter | solution.py:306
  44.5 238.0 %copy-start.81 = (f32[512]{0:T(512)}, f32[512]{0:T(512)S(1)}, u32[]{:S(2)}) copy-start(f32[512]{0:T(512)S(1)} %get-tuple-element.101) | copy-start | bytes 6148
  67.8 193.3 %copy-start.39 = (bf16[196,512]{1,0:T(8,128)(2,1)}, bf16[196,512]{1,0:T(8,128)(2,1)S(1)}, u32[]{:S(2)}) copy-start(bf16[196,512]{1,0:T(8,128)(2,1)S(1)} %reshape_reshape.24) | copy-start | bytes 602116
  450.9 121.3 %reduce-scatter.31.cloned.1.call-start = ((), (), s32[]{:S(2)}) async-start(), calls=%async_computation.16 | async-start | bytes 557056 | tf_op jit(solution)/shard_map/reduce_scatter | solution.py:306
  460.2 166.5 %reduce-scatter.27.cloned.1.call-start = ((), (), s32[]{:S(2)}) async-start(), calls=%async_computation.14 | async-start | bytes 1671168 | tf_op jit(solution)/shard_map/reduce_scatter | solution.py:303
  466.2 223.0 %reduce-scatter.29.cloned.1.call-start = ((), (), s32[]{:S(2)}) async-start(), calls=%async_computation.15 | async-start | bytes 1671168 | tf_op jit(solution)/shard_map/reduce_scatter | solution.py:303
  468.1 285.4 %reduce-scatter.37.cloned.1.call-start = ((), (), s32[]{:S(2)}) async-start(), calls=%async_computation.19 | async-start | bytes 2228224 | tf_op jit(solution)/shard_map/reduce_scatter | solution.py:320
  471.4 346.8 %reduce-scatter.35.cloned.1.call-start = ((), (), s32[]{:S(2)}) async-start(), calls=%async_computation.18 | async-start | bytes 2228224 | tf_op jit(solution)/shard_map/reduce_scatter | solution.py:320
  474.6 407.8 %reduce-scatter.39.cloned.1.call-start = ((), (), s32[]{:S(2)}) async-start(), calls=%async_computation.20 | async-start | bytes 2228224 | tf_op jit(solution)/shard_map/reduce_scatter | solution.py:323
  478.0 469.1 %reduce-scatter.41.cloned.1.call-start = ((), (), s32[]{:S(2)}) async-start(), calls=%async_computation.21 | async-start | bytes 2228224 | tf_op jit(solution)/shard_map/reduce_scatter | solution.py:323
  481.4 523.2 %reduce-scatter.47.cloned.1.call-start = ((), (), s32[]{:S(2)}) async-start(), calls=%async_computation.30 | async-start | bytes 139264
  496.8 565.2 %reduce-scatter.49.cloned.1.call-start = ((), (), s32[]{:S(2)}) async-start(), calls=%async_computation.31 | async-start | bytes 139264
  529.4 590.0 %reduce-scatter.43.cloned.1.call-start = ((), (), s32[]{:S(2)}) async-start(), calls=%async_computation.28 | async-start | bytes 139264
  530.4 647.1 %reduce-scatter.45.cloned.1.call-start = ((), (), s32[]{:S(2)}) async-start(), calls=%async_computation.29 | async-start | bytes 139264
  531.8 703.2 %reduce-scatter.51.cloned.1.call-start = ((), (), s32[]{:S(2)}) async-start(), calls=%async_computation.32 | async-start | bytes 139264
  533.6 415.3 %copy-start.34 = (f32[1,14,14,512]{3,0,2,1:T(1,128)S(1)}, f32[1,14,14,512]{3,0,2,1:T(1,128)}, u32[]{:S(2)}) copy-start(f32[1,14,14,512]{3,0,2,1:T(1,128)} %get-tuple-element.127) | copy-start | bytes 1204228
  534.3 758.2 %reduce-scatter.53.cloned.1.call-start = ((), (), s32[]{:S(2)}) async-start(), calls=%async_computation.33 | async-start | bytes 139264
  572.1 757.3 %all-reduce.7.cloned.1.call-start = ((), (), s32[]{:S(2)}) async-start(), calls=%async_computation.34 | async-start | bytes 1572864 | tf_op jit(solution)/shard_map/psum | solution.py:73
  (113 other events, 1343.8 us)
Sparse Core Ops, SparseCore 0:
  10.9 42.7 all-gather.22
  56.4 40.3 all-gather.24
  99.5 40.4 all-gather.26
  142.1 38.9 all-gather.28
  183.7 40.5 all-gather.30
  226.9 40.4 all-gather.32
  451.1 53.9 reduce-scatter.32
  509.6 54.7 reduce-scatter.30
  568.1 58.5 reduce-scatter.26
  630.6 58.4 reduce-scatter.28
  692.9 60.5 reduce-scatter.36
  757.6 60.5 reduce-scatter.34
  821.9 60.4 reduce-scatter.38
  886.5 60.5 reduce-scatter.40
  950.4 54.0 reduce-scatter.46
  1007.8 54.1 reduce-scatter.48
  1065.3 54.0 reduce-scatter.42
  1123.3 54.0 reduce-scatter.44
  1180.9 54.0 reduce-scatter.50
  1238.3 54.0 reduce-scatter.52
  1295.5 33.8 all-reduce.6
where the time goes:
time: 1350 us; the launch traced here: 1340 us
  waiting for transfers between devices  739 us (55%)
  blocking collectives  284 us (21%)
  local copies, waits for them, and re-layouts  132 us (10%)
  other arithmetic  84.2 us (6%)
  matrix products  84.1 us (6%)
  between operations  17.4 us (1%)
    unnamed x27, waiting for transfers between devices  340 us
    reduce_scatter x2, waiting for transfers between devices, body(): lax.psum_scatter(grad_w_first.astype(jnp.bfloat16), 'shard', scatter_dime...  127 us
    reduce_scatter x2, waiting for transfers between devices, body(): lax.psum_scatter(grad_w_second.astype(jnp.bfloat16), 'shard', scatter_dim...  127 us
    reduce_scatter x2, waiting for transfers between devices, body(): lax.psum_scatter(grad_w_proj_qkv.astype(jnp.bfloat16), 'shard', scatter_d...  116 us
    all_gather x2, blocking collectives, body(): lax.all_gather(branch_biases[layer_num], 'shard', axis=1, tiled=True)  52.1 us
    all_gather x2, blocking collectives, body(): lax.all_gather(norm_gains[layer_num], 'shard', axis=1, tiled=True)  42.1 us
    all_gather x2, blocking collectives, body(): lax.all_gather(w_proj[layer_num], 'shard', axis=0, tiled=True)  41.2 us
    all_gather x2, blocking collectives, body(): lax.all_gather(norm_shifts[layer_num], 'shard', axis=1, tiled=True)  37.8 us
  transfers between devices with their start and end apart: 21, of which 13 were waited for; matrix products, arithmetic and copies ran while one was open for 13% of the time, Pallas kernels for 0%

commit v1 on v0

--- a/solution.py
+++ b/solution.py
@@ -1,3 +1,5 @@
+import functools
+
 import jax
 import jax.numpy as jnp
 from jax import lax
@@ -6,6 +8,7 @@
 SIDE = 14
 WIN = 7
 SHIFT = 3
+PAD_ROWS = 16
 
 
 eps = 1e-05
@@ -68,16 +71,101 @@
     return (rel_index[:, None] == jnp.arange(table_side * table_side)[None, :]).astype(jnp.float32)
 
 
-def replica_total(stacked):
+def pack_local(w_qkv, w_proj, w_fc1, w_fc2, gains, shifts, biases, fc1_bias):
+    width = w_proj.shape[1]
+    blocks = [w_qkv[:, n * width : (n + 1) * width] for n in range(w_qkv.shape[1] // width)]
+    blocks.append(w_proj)
+    blocks += [w_fc1[:, n * width : (n + 1) * width] for n in range(w_fc1.shape[1] // width)]
+    blocks.append(w_fc2)
+    small = jnp.concatenate(
+        [gains.reshape(-1), shifts.reshape(-1), biases.reshape(-1), fc1_bias.reshape(-1)]
+    )
+    small = jnp.pad(small, (0, width - small.shape[0])).reshape(1, width)
+    blocks.append(jnp.pad(small, ((0, PAD_ROWS - 1), (0, 0))))
+    return jnp.concatenate(blocks, axis=0)
+
+
+def unpack_gathered(packed, w_qkv, w_fc1, w_fc2):
+    shard_count, _, width = packed.shape
+    rows = w_qkv.shape[0]
+    full = rows * shard_count
+
+    def piece(n):
+        return packed[:, n * rows : (n + 1) * rows].reshape(full, width)
+
+    qkv_parts = w_qkv.shape[1] // width
+    fc1_parts = w_fc1.shape[1] // width
+    wqkv = jnp.concatenate([piece(n) for n in range(qkv_parts)], axis=1)
+    wproj = piece(qkv_parts)
+    wfirst = jnp.concatenate([piece(qkv_parts + 1 + n) for n in range(fc1_parts)], axis=1)
+    start = (qkv_parts + 1 + fc1_parts) * rows
+    wsecond = packed[:, start : start + w_fc2.shape[0]].reshape(-1, width)
+    small = packed[:, start + w_fc2.shape[0]]
+
+    def vectors(first, count):
+        part = small[:, first : first + count * rows].reshape(shard_count, count, rows)
+        return jnp.swapaxes(part, 0, 1).reshape(count, full)
+
+    gains, shifts, biases = vectors(0, 2), vectors(2 * rows, 2), vectors(4 * rows, 4)
+    bias_first = small[:, 8 * rows : 8 * rows + w_fc2.shape[0]].reshape(-1)
+    return (wqkv, wproj, gains, shifts, biases), (wfirst, wsecond, bias_first)
+
+
+def pack_grads(qkv, proj, first, second, gains, shifts, biases, bias_first, shard_count):
+    width = proj.shape[1]
+
+    def rows_of(block):
+        return block.astype(jnp.bfloat16).reshape(shard_count, -1, block.shape[-1])
+
+    def vectors(block):
+        split = block.reshape(block.shape[0], shard_count, -1)
+        return jnp.swapaxes(split, 0, 1).reshape(shard_count, -1)
+
+    blocks = [rows_of(qkv[:, n * width : (n + 1) * width]) for n in range(qkv.shape[1] // width)]
+    blocks.append(rows_of(proj))
+    blocks += [rows_of(first[:, n * width : (n + 1) * width]) for n in range(first.shape[1] // width)]
+    blocks.append(rows_of(second))
+    small = jnp.concatenate(
+        [vectors(gains), vectors(shifts), vectors(biases), bias_first.reshape(shard_count, -1)],
+        axis=1,
+    ).astype(jnp.bfloat16)
+    small = jnp.pad(small, ((0, 0), (0, width - small.shape[1])))[:, None]
+    blocks.append(jnp.pad(small, ((0, 0), (0, PAD_ROWS - 1), (0, 0))))
+    return jnp.concatenate(blocks, axis=1)
+
+
+def rep_sum(share, rep_count):
+    total = share
+    step = 1
+    while step < rep_count:
+        pairs = [(n, n ^ step) for n in range(rep_count)]
+        total = total + lax.ppermute(total, "rep", pairs)
+        step *= 2
+    return total
+
+
+def unpack_shares(shares, w_qkv, w_fc2, fc1_bias):
+    shares = shares.astype(jnp.float32)
+    layer_count, _, width = shares.shape
+    rows = w_qkv.shape[1]
+    hidden = fc1_bias.shape[1]
+    qkv_parts = w_qkv.shape[2] // width
+    fc1_parts = (shares.shape[1] - PAD_ROWS - w_fc2.shape[1]) // rows - qkv_parts - 1
+
+    def piece(n):
+        return shares[:, n * rows : (n + 1) * rows]
+
+    start = (qkv_parts + 1 + fc1_parts) * rows
+    small = shares[:, start + w_fc2.shape[1]]
     return (
-        lax.psum(stacked[0].astype(jnp.bfloat16), "rep").astype(jnp.float32),
-        lax.psum(stacked[1].astype(jnp.bfloat16), "rep").astype(jnp.float32),
-        lax.psum(stacked[2].astype(jnp.bfloat16), "rep").astype(jnp.float32),
-        lax.psum(stacked[3].astype(jnp.bfloat16), "rep").astype(jnp.float32),
-        lax.psum(stacked[4].astype(jnp.bfloat16), "rep").astype(jnp.float32),
-        lax.psum(stacked[5].astype(jnp.bfloat16), "rep").astype(jnp.float32),
-        lax.psum(stacked[6].astype(jnp.bfloat16), "rep").astype(jnp.float32),
-        lax.psum(stacked[7].astype(jnp.bfloat16), "rep").astype(jnp.float32),
+        jnp.concatenate([piece(n) for n in range(qkv_parts)], axis=2),
+        piece(qkv_parts),
+        jnp.concatenate([piece(qkv_parts + 1 + n) for n in range(fc1_parts)], axis=2),
+        shares[:, start : start + w_fc2.shape[1]],
+        small[:, : 2 * rows].reshape(layer_count, 2, rows),
+        small[:, 2 * rows : 4 * rows].reshape(layer_count, 2, rows),
+        small[:, 4 * rows : 8 * rows].reshape(layer_count, 4, rows),
+        small[:, 8 * rows : 8 * rows + hidden],
     )
 
 
@@ -94,6 +182,8 @@
     branch_biases,
     fc1_bias,
     rel_table,
+    rep_count,
+    shard_count,
 ):
     layer_count = w_qkv.shape[0]
     image_count = images.shape[0]
@@ -125,24 +215,22 @@
     def heads_of(flat):
         return flat.reshape(window_count, WIN * WIN, head_count, head_dim)
 
+    gathered = []
+    for layer_num in range(layer_count):
+        own = pack_local(
+            w_qkv[layer_num], w_proj[layer_num], w_fc1[layer_num], w_fc2[layer_num],
+            norm_gains[layer_num], norm_shifts[layer_num], branch_biases[layer_num],
+            fc1_bias[layer_num],
+        )
+        packed = lax.all_gather(own, "shard", axis=0, tiled=False)
+        gathered.append(
+            unpack_gathered(packed, w_qkv[layer_num], w_fc1[layer_num], w_fc2[layer_num])
+        )
     residual = images.astype(jnp.float32)
     saved_acts = []
-    kept_weights = []
     for layer_num in range(layer_count):
         shifted = layer_num % 2 == 1
-        attn_w = (
-            lax.all_gather(w_qkv[layer_num], "shard", axis=0, tiled=True),
-            lax.all_gather(w_proj[layer_num], "shard", axis=0, tiled=True),
-            lax.all_gather(norm_gains[layer_num], "shard", axis=1, tiled=True),
-            lax.all_gather(norm_shifts[layer_num], "shard", axis=1, tiled=True),
-            lax.all_gather(branch_biases[layer_num], "shard", axis=1, tiled=True),
-        )
-        mlp_w = (
-            lax.all_gather(w_fc1[layer_num], "shard", axis=0, tiled=True),
-            lax.all_gather(w_fc2[layer_num], "shard", axis=0, tiled=True),
-            lax.all_gather(fc1_bias[layer_num], "shard", axis=0, tiled=True),
-        )
-        kept_weights.append((attn_w, mlp_w))
+        attn_w, mlp_w = gathered[layer_num]
         wqkv, wproj, gains, shifts, biases = attn_w
         gains = gains.astype(jnp.float32)
         shifts = shifts.astype(jnp.float32)
@@ -199,7 +287,7 @@
         residual = middle + mlp_out.reshape(middle.shape)
     images_out = residual.astype(jnp.bfloat16)
     upstream = cotangent.astype(jnp.float32)
-    layer_grads = [None] * layer_count
+    shares = [None] * layer_count
     table_list = [None] * layer_count
     for layer_num in reversed(range(layer_count)):
         shifted = layer_num % 2 == 1
@@ -216,18 +304,7 @@
             pre_act,
             activated,
         ) = saved_acts[layer_num]
-        wqkv, wproj, gains, shifts, biases = (
-            lax.all_gather(w_qkv[layer_num], "shard", axis=0, tiled=True),
-            lax.all_gather(w_proj[layer_num], "shard", axis=0, tiled=True),
-            lax.all_gather(norm_gains[layer_num], "shard", axis=1, tiled=True),
-            lax.all_gather(norm_shifts[layer_num], "shard", axis=1, tiled=True),
-            lax.all_gather(branch_biases[layer_num], "shard", axis=1, tiled=True),
-        )
-        wfirst, wsecond, bias_first = (
-            lax.all_gather(w_fc1[layer_num], "shard", axis=0, tiled=True),
-            lax.all_gather(w_fc2[layer_num], "shard", axis=0, tiled=True),
-            lax.all_gather(fc1_bias[layer_num], "shard", axis=0, tiled=True),
-        )
+        (wqkv, wproj, gains, shifts, biases), (wfirst, wsecond, bias_first) = gathered[layer_num]
         gains = gains.astype(jnp.float32)
         shifts = shifts.astype(jnp.float32)
         out_grad = upstream.astype(jnp.bfloat16).reshape(-1, model_width)
@@ -299,46 +376,14 @@
         gain_grads = jnp.stack([grad_gain_attn, grad_gain_mlp])
         shift_grads = jnp.stack([grad_shift_attn, grad_shift_mlp])
         bias_grads = jnp.stack([grad_b_query, grad_b_value, grad_b_proj, grad_b_second])
-        qkv_share, proj_share, gain_share, shift_share, bias_share = (
-            lax.psum_scatter(
-                grad_w_proj_qkv.astype(jnp.bfloat16), "shard", scatter_dimension=0, tiled=True
-            ).astype(jnp.float32),
-            lax.psum_scatter(
-                grad_w_proj.astype(jnp.bfloat16), "shard", scatter_dimension=0, tiled=True
-            ).astype(jnp.float32),
-            lax.psum_scatter(
-                gain_grads.astype(jnp.bfloat16), "shard", scatter_dimension=1, tiled=True
-            ).astype(jnp.float32),
-            lax.psum_scatter(
-                shift_grads.astype(jnp.bfloat16), "shard", scatter_dimension=1, tiled=True
-            ).astype(jnp.float32),
-            lax.psum_scatter(
-                bias_grads.astype(jnp.bfloat16), "shard", scatter_dimension=1, tiled=True
-            ).astype(jnp.float32),
-        )
-        first_share, second_share, bfirst_share = (
-            lax.psum_scatter(
-                grad_w_first.astype(jnp.bfloat16), "shard", scatter_dimension=0, tiled=True
-            ).astype(jnp.float32),
-            lax.psum_scatter(
-                grad_w_second.astype(jnp.bfloat16), "shard", scatter_dimension=0, tiled=True
-            ).astype(jnp.float32),
-            lax.psum_scatter(
-                grad_b_first.astype(jnp.bfloat16), "shard", scatter_dimension=0, tiled=True
-            ).astype(jnp.float32),
-        )
-        layer_grads[layer_num] = (
-            qkv_share,
-            proj_share,
-            first_share,
-            second_share,
-            gain_share,
-            shift_share,
-            bias_share,
-            bfirst_share,
-        )
-    stacked = [jnp.stack([layer_grads[n][m] for n in range(layer_count)]) for m in range(8)]
-    summed = replica_total(stacked)
+        packed_grads = pack_grads(
+            grad_w_proj_qkv, grad_w_proj, grad_w_first, grad_w_second,
+            gain_grads, shift_grads, bias_grads, grad_b_first, shard_count,
+        )
+        shares[layer_num] = lax.psum_scatter(
+            packed_grads, "shard", scatter_dimension=0, tiled=False
+        )
+    summed = unpack_shares(rep_sum(jnp.stack(shares), rep_count), w_qkv, w_fc2, fc1_bias)
     table_total = lax.psum(jnp.stack(table_list), ("rep", "shard"))
     return (
         images_out,
@@ -357,7 +402,9 @@
 
 def solution(mesh):
     return jax.shard_map(
-        body,
+        functools.partial(
+            body, rep_count=mesh.shape["rep"], shard_count=mesh.shape["shard"]
+        ),
         mesh=mesh,
         in_specs=(
             P(("rep", "shard"), None, None, None),

time: 1350 us -> 647 us (0.48)
  waiting for transfers between devices: 739 us -> 279 us
  blocking collectives: 284 us -> 50.3 us
  local copies, waits for them, and re-layouts: 132 us -> 152 us
  other arithmetic: 84.2 us -> 67.1 us
    unnamed x27 -> x4, waiting for transfers between devices: 340 us -> 0.07 us
    reduce_scatter x8 -> x2, waiting for transfers between devices: 370 us -> 157 us  [body(): lax.psum_scatter(packed_grads, 'shard', scatter_dimension=0, tiled=False)]
    all_gather x10 -> x0, blocking collectives: 209 us -> none  [the longest x2 52.1 us: body(): lax.all_gather(branch_biases[layer_num], 'shard', axis=1, tiled=True)]
    all_gather x6 -> x2, waiting for transfers between devices: 0.05 us -> 122 us  [body(): packed = lax.all_gather(own, 'shard', axis=0, tiled=False)]
    unnamed x1 -> x0, blocking collectives: 31.7 us -> none
    psum x1 -> x0, waiting for transfers between devices: 28.8 us -> none  [replica_total(): lax.psum(stacked[0].astype(jnp.bfloat16), 'rep').astype(jnp.float32)]
    unnamed x252 -> x290, local copies, waits for them, and re-layouts: 20 us -> 30.6 us
  transfers between devices with their start and end apart: 21 -> 5, of which waited for: 13 -> 4; matrix products, arithmetic and copies ran while one was open for 13% -> 5% of each run, Pallas kernels for 0% -> 0%
where the time goes in v1:
time: 647 us; the launch traced here: 640 us
  waiting for transfers between devices  279 us (43%)
  local copies, waits for them, and re-layouts  152 us (23%)
  matrix products  74.3 us (11%)
  other arithmetic  67.1 us (10%)
  blocking collectives  50.3 us (8%)
  between operations  16 us (2%)
    reduce_scatter x2, waiting for transfers between devices, body(): lax.psum_scatter(packed_grads, 'shard', scatter_dimension=0, tiled=False)  157 us
    all_gather x2, waiting for transfers between devices, body(): packed = lax.all_gather(own, 'shard', axis=0, tiled=False)  122 us
    psum x1, blocking collectives, body(): table_total = lax.psum(jnp.stack(table_list), ('rep', 'shard'))  50.3 us
    unnamed x290, local copies, waits for them, and re-layouts  30.6 us
    reshape x16, local copies, waits for them, and re-layouts, heads_of(): return flat.reshape(window_count, WIN * WIN, head_count, head_dim)  27.9 us
    dot_general x10, matrix products, times_transposed(): lax.dot_general(left, right, (((1,), (1,)), ((), ())), preferred_element_...  23.3 us
    reduce_sum x6, other arithmetic, layer_norm(): return centred * lax.rsqrt(row_var + eps) * norm_gain + norm_shift  17 us
    reduce_sum x4, other arithmetic, layer_norm(): centred = values - row_mean  15.5 us
  transfers between devices with their start and end apart: 5, of which 4 were waited for; matrix products, arithmetic and copies ran while one was open for 5% of the time, Pallas kernels for 0%

profile of v1, /device:TPU:0, one launch (start us, length us, event | category | flops | bytes accessed | tf_op | source)
XLA Modules:
  0.0 640.2 jit_solution(6464337285100366008)
XLA Ops:
  21.9 58.8 %all-gather.7.cloned.1.call-done = bf16[6400,512]{1,0:T(8,128)(2,1)} async-done(((bf16[400,512]{1,0:T(8,128)(2,1)}), bf16[6400,512]{1,0:T(8,128)(2,1)}) %all-gather.7.cloned.1.call-update) | async-done | bytes 6553616 | tf_op jit(solution)/shard_map/all_gather | solution.py:225
  82.3 63.2 %all-gather.5.cloned.1.call-done = bf16[6400,512]{1,0:T(8,128)(2,1)} async-done(((bf16[400,512]{1,0:T(8,128)(2,1)}), bf16[6400,512]{1,0:T(8,128)(2,1)}) %all-gather.5.cloned.1.call-update) | async-done | bytes 6553616 | tf_op jit(solution)/shard_map/all_gather | solution.py:225
  146.6 3.2 slice.594
  149.8 4.1 fusion.168
  183.8 7.5 %fusion.9 = (bf16[196,2048]{1,0:T(8,128)(2,1)S(1)}, f32[196,2048]{1,0:T(8,128)}) fusion(f32[2048]{0:T(1024)S(1)} %get-tuple-element.177, bf16[196,512]{1,0:T(8,128)(2,1)S(1)} %reshape.980, bf16[512,512]{1,0:T(8,128)(2,1)} %bitcast.295, bf16[512,512]{1,0:T(8,128)(2,1)} %bitcast.297, bf16[512,512]{1,0:T(8,128)(2,1)} %bitcast.299, bf16[512,512]{1,0:T(8,128)(2,1)} %bitcast.293), kind=kOutput, calls=%fused_computation.39 | convolution fusion | flops 445923328 | bytes 4714496 | tf_op jit(solution)/shard_map/dot_general | solution.py:267
  212.5 2.7 copy.352
  242.3 7.2 %fusion.12 = (bf16[196,2048]{1,0:T(8,128)(2,1)S(1)}, f32[196,2048]{1,0:T(8,128)}) fusion(f32[2048]{0:T(1024)} %get-tuple-element.173, bf16[196,512]{1,0:T(8,128)(2,1)} %reshape.998, bf16[512,512]{1,0:T(8,128)(2,1)} %bitcast.307, bf16[512,512]{1,0:T(8,128)(2,1)} %bitcast.309, bf16[512,512]{1,0:T(8,128)(2,1)} %bitcast.311, bf16[512,512]{1,0:T(8,128)(2,1)} %bitcast.305), kind=kOutput, calls=%fused_computation.42 | convolution fusion | flops 445923328 | bytes 4714496 | tf_op jit(solution)/shard_map/dot_general | solution.py:267
  254.0 4.0 fusion.184
  262.4 4.7 multiply_reduce_fusion.2
  267.1 5.2 fusion.161
  289.2 3.1 fusion.185
  310.5 2.6 convolution_add_fusion.3
  318.5 4.1 multiply_reduce_fusion.3
  322.7 3.4 fusion.160
  328.3 3.9 fusion.180
  336.0 3.1 multiply_reduce_fusion.4
  339.1 3.6 fusion.159
  342.7 2.8 convert_reduce_fusion.4
  372.4 2.6 fusion.183
  376.8 3.3 multiply_reduce_fusion.5
  411.0 67.9 %reduce-scatter.3.cloned.1.call-done = bf16[1,400,512]{2,1,0:T(8,128)(2,1)} async-done(((bf16[16,400,512]{2,1,0:T(8,128)(2,1)}), bf16[1,400,512]{2,1,0:T(8,128)(2,1)}) %reduce-scatter.3.cloned.1.call-update) | async-done | bytes 409616 | tf_op jit(solution)/shard_map/reduce_scatter | solution.py:383
  480.0 89.2 %reduce-scatter.5.cloned.1.call-done = bf16[1,400,512]{2,1,0:T(8,128)(2,1)} async-done(((bf16[16,400,512]{2,1,0:T(8,128)(2,1)}), bf16[1,400,512]{2,1,0:T(8,128)(2,1)}) %reduce-scatter.5.cloned.1.call-update) | async-done | bytes 409616 | tf_op jit(solution)/shard_map/reduce_scatter | solution.py:383
  572.5 50.3 %psum.7 = f32[2,169,16]{1,2,0:T(8,128)} all-reduce(f32[2,169,16]{1,2,0:T(8,128)S(1)} %pad_maximum_fusion.14), channel_id=1, replica_groups=mesh['rep'=2,'shard'=16] {'rep','shard'}, use_global_device_ids=true, to_apply=%region_45.46 | all-reduce | flops 5408 | bytes 43264 | tf_op jit(solution)/shard_map/psum | solution.py:387
  622.8 3.4 fusion.158
  (577 shorter events, 220.2 us)
Async XLA Ops:
  7.2 73.5 %all-gather.7.cloned.1.call-start = ((), (), s32[]{:S(2)}) async-start(), calls=%async_computation.5 | async-start | bytes 6963200 | tf_op jit(solution)/shard_map/all_gather | solution.py:225
  14.5 131.1 %all-gather.5.cloned.1.call-start = ((), (), s32[]{:S(2)}) async-start(), calls=%async_computation.4 | async-start | bytes 6963200 | tf_op jit(solution)/shard_map/all_gather | solution.py:225
  15.3 463.6 %reduce-scatter.3.cloned.1.call-start = ((), (), s32[]{:S(2)}) async-start(), calls=%async_computation.2 | async-start | bytes 6963200 | tf_op jit(solution)/shard_map/reduce_scatter | solution.py:383
  20.1 140.1 %copy-start.71 = (f32[14,14]{1,0:T(8,128)}, f32[14,14]{1,0:T(8,128)S(1)}, u32[]{:S(2)}) copy-start(f32[14,14]{1,0:T(8,128)S(1)} %broadcast_multiply_fusion.3) | copy-start | bytes 2356
  21.1 59.6 %copy-start.83 = (f32[14,14]{1,0:T(8,128)}, f32[14,14]{1,0:T(8,128)S(1)}, u32[]{:S(2)}) copy-start(f32[14,14]{1,0:T(8,128)S(1)} %multiply_reduce_fusion.13) | copy-start | bytes 2356
  21.1 139.1 %copy-start.80 = (f32[14,14]{1,0:T(8,128)}, f32[14,14]{1,0:T(8,128)S(1)}, u32[]{:S(2)}) copy-start(f32[14,14]{1,0:T(8,128)S(1)} %fusion.121) | copy-start | bytes 2356
  153.9 8.4 %copy-start.20 = (bf16[16,32,512]{2,1,0:T(8,128)(2,1)}, bf16[16,32,512]{2,1,0:T(8,128)(2,1)S(1)}, u32[]{:S(2)}) copy-start(bf16[16,32,512]{2,1,0:T(8,128)(2,1)S(1)} %get-tuple-element.135) | copy-start | bytes 1572868
  153.9 23.1 %copy-start.5 = (bf16[16,32,512]{2,1,0:T(8,128)(2,1)}, bf16[16,32,512]{2,1,0:T(8,128)(2,1)S(1)}, u32[]{:S(2)}) copy-start(bf16[16,32,512]{2,1,0:T(8,128)(2,1)S(1)} %get-tuple-element.132) | copy-start | bytes 1572868
  158.4 39.0 %copy-start.94 = (f32[512]{0:T(512)}, f32[512]{0:T(512)S(1)}, u32[]{:S(2)}) copy-start(f32[512]{0:T(512)S(1)} %mul.494) | copy-start | bytes 6148
  159.4 22.4 %copy-start.92 = (f32[512]{0:T(512)}, f32[512]{0:T(512)S(1)}, u32[]{:S(2)}) copy-start(f32[512]{0:T(512)S(1)} %mul.485) | copy-start | bytes 6148
  183.8 7.6 %copy-start.41 = (bf16[196,512]{1,0:T(8,128)(2,1)}, bf16[196,512]{1,0:T(8,128)(2,1)S(1)}, u32[]{:S(2)}) copy-start(bf16[196,512]{1,0:T(8,128)(2,1)S(1)} %reshape.980) | copy-start | bytes 602116
  183.8 8.5 %copy-start.22 = (bf16[16,128,512]{2,1,0:T(8,128)(2,1)S(1)}, bf16[16,128,512]{2,1,0:T(8,128)(2,1)}, u32[]{:S(2)}) copy-start(bf16[16,128,512]{2,1,0:T(8,128)(2,1)} %slice.594) | copy-start | bytes 6291460
  226.5 7.9 %copy-start.98 = (f32[16,32]{1,0:T(8,128)S(1)}, f32[16,32]{1,0:T(8,128)}, u32[]{:S(2)}) copy-start(f32[16,32]{1,0:T(8,128)} %get-tuple-element.88) | copy-start | bytes 6148
  226.5 8.6 %copy-start.99 = (f32[16,32]{1,0:T(8,128)S(1)}, f32[16,32]{1,0:T(8,128)}, u32[]{:S(2)}) copy-start(f32[16,32]{1,0:T(8,128)} %get-tuple-element.78) | copy-start | bytes 6148
  242.3 8.2 %copy-start.23 = (bf16[16,128,512]{2,1,0:T(8,128)(2,1)S(1)}, bf16[16,128,512]{2,1,0:T(8,128)(2,1)}, u32[]{:S(2)}) copy-start(bf16[16,128,512]{2,1,0:T(8,128)(2,1)} %slice.632) | copy-start | bytes 6291460
  242.3 8.2 %copy-start.117 = (f32[512]{0:T(512)S(1)}, f32[512]{0:T(512)}, u32[]{:S(2)}) copy-start(f32[512]{0:T(512)} %add.435) | copy-start | bytes 6148
  262.4 9.9 %copy-start.26 = (bf16[1,14,14,512]{3,2,1,0:T(8,128)(2,1)S(1)}, bf16[1,14,14,512]{3,2,1,0:T(8,128)(2,1)}, u32[]{:S(2)}) copy-start(bf16[1,14,14,512]{3,2,1,0:T(8,128)(2,1)} %param.13) | copy-start | bytes 602116
  334.4 8.3 %copy-start.34 = (f32[1,14,14,512]{3,0,2,1:T(1,128)S(1)}, f32[1,14,14,512]{3,0,2,1:T(1,128)}, u32[]{:S(2)}) copy-start(f32[1,14,14,512]{3,0,2,1:T(1,128)} %get-tuple-element.109) | copy-start | bytes 1204228
  393.3 175.9 %reduce-scatter.5.cloned.1.call-start = ((), (), s32[]{:S(2)}) async-start(), calls=%async_computation.3 | async-start | bytes 6963200 | tf_op jit(solution)/shard_map/reduce_scatter | solution.py:383
  409.1 162.7 %copy-start.32 = (bf16[1,14,14,512]{3,0,2,1:T(2,128)(2,1)S(1)}, bf16[1,14,14,512]{3,0,2,1:T(2,128)(2,1)}, u32[]{:S(2)}) copy-start(bf16[1,14,14,512]{3,0,2,1:T(2,128)(2,1)} %get-tuple-element.164) | copy-start | bytes 602116
  410.1 212.7 %copy-start.82 = (f32[14,14]{1,0:T(8,128)S(1)}, f32[14,14]{1,0:T(8,128)}, u32[]{:S(2)}) copy-start(f32[14,14]{1,0:T(8,128)} %copy-done.80) | copy-start | bytes 2356
  410.1 212.7 %copy-start.91 = (f32[512]{0:T(512)S(1)}, f32[512]{0:T(512)}, u32[]{:S(2)}) copy-start(f32[512]{0:T(512)} %copy-done.89) | copy-start | bytes 6148
  411.0 215.2 %copy-start.33 = (f32[1,14,14,512]{3,0,2,1:T(1,128)S(1)}, f32[1,14,14,512]{3,0,2,1:T(1,128)}, u32[]{:S(2)}) copy-start(f32[1,14,14,512]{3,0,2,1:T(1,128)} %get-tuple-element.106) | copy-start | bytes 1204228
  570.2 57.2 %collective-permute-start = (bf16[2,400,512]{2,1,0:T(8,128)(2,1)S(1)}, bf16[2,400,512]{2,1,0:T(8,128)(2,1)S(1)}, u32[]{:S(2)}, u32[]{:S(2)}) collective-permute-start(bf16[2,400,512]{2,1,0:T(8,128)(2,1)S(1)} %constant_dynamic-update-slice_fusion.36), channel_id=1, source_target_pairs={{0,16},{16,0},{1,17},{17,1},{2,18},{18,2},{3,19},{19,3},{4,20},{20... | collective-permute-start | bytes 2457608 | tf_op jit(solution)/shard_map/ppermute | solution.py:142
  (106 other events, 285.0 us)
Sparse Core Ops, SparseCore 0:
  14.6 66.0 all-gather.6
  83.6 61.9 all-gather.4
  393.4 85.4 reduce-scatter.2
  483.3 85.9 reduce-scatter.4

commit v2 on v1

v2 whole, which is shorter than its diff:
```python
import functools

import jax
import jax.numpy as jnp
import numpy as np
from jax import lax
from jax.experimental import pallas as pl
from jax.experimental.pallas import tpu as pltpu
from jax.sharding import PartitionSpec as P

SIDE = 14
WIN = 7
SHIFT = 3
PAD_ROWS = 16
CELLS = WIN * WIN
SLOT = 64
WINDOWS = (SIDE // WIN) ** 2
TOKENS = WINDOWS * SLOT
LANES = 128

eps = 1e-05
highest = lax.Precision.HIGHEST
inv_root_two = 0.7071067811865476
inv_root_two_pi = 0.3989422804014327


def to_windows(grid_data):
    image_count = grid_data.shape[0]
    per_side = SIDE // WIN
    trailing = grid_data.shape[3:]
    blocks = grid_data.reshape((image_count, per_side, WIN, per_side, WIN) + trailing)
    blocks = jnp.swapaxes(blocks, 2, 3)
    return blocks.reshape((image_count * per_side * per_side, WIN * WIN) + trailing)


def from_windows(blocks, image_count):
    per_side = SIDE // WIN
    trailing = blocks.shape[2:]
    grid_data = blocks.reshape((image_count, per_side, per_side, WIN, WIN) + trailing)
    grid_data = jnp.swapaxes(grid_data, 2, 3)
    return grid_data.reshape((image_count, SIDE, SIDE) + trailing)


def pack_local(w_qkv, w_proj, w_fc1, w_fc2, gains, shifts, biases, fc1_bias):
    width = w_proj.shape[1]
    blocks = [w_qkv[:, n * width : (n + 1) * width] for n in range(w_qkv.shape[1] // width)]
    blocks.append(w_proj)
    blocks += [w_fc1[:, n * width : (n + 1) * width] for n in range(w_fc1.shape[1] // width)]
    blocks.append(w_fc2)
    small = jnp.concatenate(
        [gains.reshape(-1), shifts.reshape(-1), biases.reshape(-1), fc1_bias.reshape(-1)]
    )
    small = jnp.pad(small, (0, width - small.shape[0])).reshape(1, width)
    blocks.append(jnp.pad(small, ((0, PAD_ROWS - 1), (0, 0))))
    return jnp.concatenate(blocks, axis=0)


def rep_sum(share, rep_count):
    total = share
    step = 1
    while step < rep_count:
        pairs = [(n, n ^ step) for n in range(rep_count)]
        total = total + lax.ppermute(total, "rep", pairs)
        step *= 2
    return total


def unpack_shares(shares, w_qkv, w_fc2, fc1_bias):
    shares = shares.astype(jnp.float32)
    layer_count, _, width = shares.shape
    rows = w_qkv.shape[1]
    hidden = fc1_bias.shape[1]
    qkv_parts = w_qkv.shape[2] // width
    fc1_parts = (shares.shape[1] - PAD_ROWS - w_fc2.shape[1]) // rows - qkv_parts - 1

    def piece(n):
        return shares[:, n * rows : (n + 1) * rows]

    start = (qkv_parts + 1 + fc1_parts) * rows
    small = shares[:, start + w_fc2.shape[1]]
    return (
        jnp.concatenate([piece(n) for n in range(qkv_parts)], axis=2),
        piece(qkv_parts),
        jnp.concatenate([piece(qkv_parts + 1 + n) for n in range(fc1_parts)], axis=2),
        shares[:, start : start + w_fc2.shape[1]],
        small[:, : 2 * rows].reshape(layer_count, 2, rows),
        small[:, 2 * rows : 4 * rows].reshape(layer_count, 2, rows),
        small[:, 4 * rows : 8 * rows].reshape(layer_count, 4, rows),
        small[:, 8 * rows : 8 * rows + hidden],
    )


def dot(left, right):
    return jnp.dot(left, right, preferred_element_type=jnp.float32)


def dot_nt(left, right):
    return lax.dot_general(
        left, right, (((1,), (1,)), ((), ())), preferred_element_type=jnp.float32
    )


def dot_tn(left, right):
    return lax.dot_general(
        left, right, (((0,), (0,)), ((), ())), preferred_element_type=jnp.float32
    )


def normalise(values):
    row_mean = jnp.mean(values, axis=-1, keepdims=True)
    centred = values - row_mean
    rstd = lax.rsqrt(jnp.mean(centred * centred, axis=-1, keepdims=True) + eps)
    return centred * rstd, rstd


def norm_back(grad, gain, xhat, rstd):
    scaled = grad * gain
    return rstd * (
        scaled
        - jnp.mean(scaled, axis=-1, keepdims=True)
        - xhat * jnp.mean(scaled * xhat, axis=-1, keepdims=True)
    )


def low(values):
    return values.astype(jnp.bfloat16)


class Pieces:
    def __init__(self, ref, width, hidden):
        self.ref = ref
        self.width = width
        self.shards = ref.shape[0]
        self.rows = width // self.shards
        self.hidden = hidden // self.shards
        self.parts = hidden // width
        self.start = (4 + self.parts) * self.rows

    def square(self, n):
        return self.ref[:, n * self.rows : (n + 1) * self.rows, :].reshape(self.width, self.width)

    def second(self, n):
        group = self.shards // self.parts
        return self.ref[
            n * group : (n + 1) * group, self.start : self.start + self.hidden, :
        ].reshape(self.width, self.width)

    def put_square(self, n, value):
        self.ref[:, n * self.rows : (n + 1) * self.rows, :] = low(value).reshape(
            self.shards, self.rows, self.width
        )

    def put_second(self, n, value):
        group = self.shards // self.parts
        self.ref[n * group : (n + 1) * group, self.start : self.start + self.hidden, :] = low(
            value
        ).reshape(group, self.hidden, self.width)


def stack_heads(block, per_group, head_dim):
    lane_head = lax.broadcasted_iota(jnp.int32, block.shape, 1) // head_dim
    zero = jnp.zeros_like(block)
    return jnp.concatenate(
        [jnp.where(lane_head == n, block, zero) for n in range(per_group)], axis=0
    )


def pick_heads(stacked, per_group, head_dim):
    rows = stacked.shape[0] // per_group
    lane_head = lax.broadcasted_iota(jnp.int32, (rows, stacked.shape[1]), 1) // head_dim
    total = stacked[:rows]
    for n in range(1, per_group):
        total = jnp.where(lane_head == n, stacked[n * rows : (n + 1) * rows], total)
    return total


def probs_of(q_stack, key_block, bias_ref, mask_ref, window, group, per_group):
    scores = dot_nt(q_stack, key_block)
    span = per_group * SLOT
    scores = scores + bias_ref[group * span : (group + 1) * span, :]
    if mask_ref is not None:
        region = mask_ref[window]
        scores = scores + jnp.concatenate([region] * per_group, axis=0)
    top = jnp.max(scores, axis=-1, keepdims=True)
    raised = jnp.exp(scores - top)
    return raised / jnp.sum(raised, axis=-1, keepdims=True)


def forward_kernel(shifted, hidden, head_dim, *refs):
    if shifted:
        (r_ref, w_ref, vec_ref, fb_ref, bias_ref, mask_ref, perm_ref, *outs) = refs
    else:
        (r_ref, w_ref, vec_ref, fb_ref, bias_ref, *outs) = refs
        mask_ref = None
    (out_ref, hs_ref, qkv_ref, mixed_ref, mid_ref, h2_ref, slope_ref, act_ref) = outs
    width = r_ref.shape[1]
    weights = Pieces(w_ref, width, hidden)
    scale = head_dim ** (-0.5)
    per_group = LANES // head_dim
    vec = lambda n: vec_ref[n : n + 1, :]
    h = low(normalise(r_ref[...])[0] * vec(0) + vec(2))
    if shifted:
        h = low(dot(perm_ref[...], h))
    hs_ref[...] = h
    qkv_ref[:, :width] = low((dot(h, weights.square(0)) + vec(4)) * scale)
    qkv_ref[:, width : 2 * width] = low(dot(h, weights.square(1)))
    qkv_ref[:, 2 * width :] = low(dot(h, weights.square(2)) + vec(5))

    def window_step(window, carry):
        rows = pl.ds(pl.multiple_of(window * SLOT, SLOT), SLOT)
        for group in range(width // LANES):
            first = group * LANES
            q_stack = stack_heads(qkv_ref[rows, first : first + LANES], per_group, head_dim)
            key_block = qkv_ref[rows, width + first : width + first + LANES]
            value_block = qkv_ref[rows, 2 * width + first : 2 * width + first + LANES]
            probs = low(
                probs_of(q_stack, key_block, bias_ref, mask_ref, window, group, per_group)
            )
            mixed_ref[rows, first : first + LANES] = low(
                pick_heads(dot(probs, value_block), per_group, head_dim)
            )
        return carry

    lax.fori_loop(0, WINDOWS, window_step, 0)
    mixed = mixed_ref[...]
    if shifted:
        mixed = low(dot_tn(perm_ref[...], mixed))
    middle = r_ref[...] + dot(mixed, weights.square(3)) + vec(6)
    mid_ref[...] = middle
    h2 = low(normalise(middle)[0] * vec(1) + vec(3))
    h2_ref[...] = h2
    out_ref[...] = middle + vec(7)
    for part in range(weights.parts):
        cols = slice(part * width, (part + 1) * width)
        pre_act = dot(h2, weights.square(4 + part)) + fb_ref[:, cols]
        half_cdf = 0.5 * (1.0 + lax.erf(pre_act * inv_root_two))
        act = low(pre_act * half_cdf)
        act_ref[:, cols] = act
        slope_ref[:, cols] = half_cdf + pre_act * inv_root_two_pi * jnp.exp(
            -0.5 * pre_act * pre_act
        )
        out_ref[...] += dot(act, weights.second(part))


def backward_kernel(shifted, hidden, head_dim, *refs):
    if shifted:
        (g_ref, w_ref, vec_ref, bias_ref, mask_ref, perm_ref, *rest) = refs
    else:
        (g_ref, w_ref, vec_ref, bias_ref, *rest) = refs
        mask_ref = None
    (r_ref, hs_ref, qkv_ref, mixed_ref, mid_ref, h2_ref, slope_ref, act_ref, *rest) = rest
    (up_ref, gw_ref, small_ref, ds_ref, dmix_ref, dqkv_ref) = rest
    width = r_ref.shape[1]
    weights = Pieces(w_ref, width, hidden)
    grads = Pieces(gw_ref, width, hidden)
    scale = head_dim ** (-0.5)
    per_group = LANES // head_dim
    vec = lambda n: vec_ref[n : n + 1, :]

    def put_sum(n, values):
        small_ref[n : n + 1, :] = jnp.sum(values.astype(jnp.float32), axis=0, keepdims=True)

    small_ref[...] = jnp.zeros_like(small_ref)
    first_spare = grads.start + grads.hidden
    gw_ref[:, first_spare:, :] = jnp.zeros(
        (grads.shards, gw_ref.shape[1] - first_spare, width), jnp.bfloat16
    )
    upstream = g_ref[...]
    out_grad = low(upstream)
    put_sum(7, out_grad)
    h2 = h2_ref[...]
    norm_grad = jnp.zeros(upstream.shape, jnp.float32)
    for part in range(weights.parts):
        cols = slice(part * width, (part + 1) * width)
        grads.put_second(part, dot_tn(act_ref[:, cols], out_grad))
        pre_grad = low(dot_nt(out_grad, weights.second(part)) * slope_ref[:, cols])
        put_sum(8 + part, pre_grad)
        grads.put_square(4 + part, dot_tn(h2, pre_grad))
        norm_grad = norm_grad + dot_nt(pre_grad, weights.square(4 + part))
    xhat, rstd = normalise(mid_ref[...])
    put_sum(1, norm_grad * xhat)
    put_sum(3, norm_grad)
    middle_grad = upstream + norm_back(norm_grad, vec(1), xhat, rstd)
    branch_grad = low(middle_grad)
    if shifted:
        branch_grad = low(dot(perm_ref[...], branch_grad))
    put_sum(6, branch_grad)
    grads.put_square(3, dot_tn(mixed_ref[...], branch_grad))
    dmix_ref[...] = low(dot_nt(branch_grad, weights.square(3)))
    ds_ref[...] = jnp.zeros_like(ds_ref)

    def window_step(window, carry):
        rows = pl.ds(pl.multiple_of(window * SLOT, SLOT), SLOT)
        for group in range(width // LANES):
            first = group * LANES
            span = per_group * SLOT
            q_stack = stack_heads(qkv_ref[rows, first : first + LANES], per_group, head_dim)
            d_stack = stack_heads(dmix_ref[rows, first : first + LANES], per_group, head_dim)
            key_block = qkv_ref[rows, width + first : width + first + LANES]
            value_block = qkv_ref[rows, 2 * width + first : 2 * width + first + LANES]
            probs = probs_of(q_stack, key_block, bias_ref, mask_ref, window, group, per_group)
            prob_grad = dot_nt(d_stack, value_block)
            value_grad = dot_tn(low(probs), d_stack)
            score_grad = low(
                probs * (prob_grad - jnp.sum(probs * prob_grad, axis=-1, keepdims=True))
            )
            ds_ref[group * span : (group + 1) * span, :] += score_grad.astype(jnp.float32)
            dqkv_ref[rows, first : first + LANES] = low(
                pick_heads(dot(score_grad, key_block), per_group, head_dim)
            )
            dqkv_ref[rows, width + first : width + first + LANES] = low(
                dot_tn(score_grad, q_stack)
            )
            dqkv_ref[rows, 2 * width + first : 2 * width + first + LANES] = low(value_grad)
        return carry

    lax.fori_loop(0, WINDOWS, window_step, 0)
    hs = hs_ref[...]
    rows_grad = jnp.zeros(upstream.shape, jnp.float32)
    for part in range(3):
        piece = dqkv_ref[:, part * width : (part + 1) * width]
        weight_grad = dot_tn(hs, piece)
        factor = scale if part == 0 else 1.0
        grads.put_square(part, weight_grad * factor)
        if part == 0:
            put_sum(4, piece.astype(jnp.float32) * scale)
        if part == 2:
            put_sum(5, piece)
        if shifted:
            piece = low(dot_tn(perm_ref[...], piece))
        rows_grad = rows_grad + dot_nt(piece, weights.square(part)) * factor
    xhat, rstd = normalise(r_ref[...])
    put_sum(0, rows_grad * xhat)
    put_sum(2, rows_grad)
    up_ref[...] = middle_grad + norm_back(rows_grad, vec(0), xhat, rstd)


def call_kernel(kernel, outs, scratch, args, flops, name):
    vmem = pl.BlockSpec(memory_space=pltpu.VMEM)
    return pl.pallas_call(
        kernel,
        out_shape=[jax.ShapeDtypeStruct(shape, kind) for shape, kind in outs],
        in_specs=[vmem] * len(args),
        out_specs=[vmem] * len(outs),
        scratch_shapes=[pltpu.VMEM(shape, kind) for shape, kind in scratch],
        compiler_params=pltpu.CompilerParams(vmem_limit_bytes=58 * 1024 * 1024),
        cost_estimate=pl.CostEstimate(flops=flops, bytes_accessed=20_000_000, transcendentals=0),
        name=name,
    )(*args)


def table_onehot():
    cell_row = np.arange(CELLS) // WIN
    cell_col = np.arange(CELLS) % WIN
    side = 2 * WIN - 1
    rel = (cell_row[:, None] - cell_row[None, :] + WIN - 1) * side + (
        cell_col[:, None] - cell_col[None, :] + WIN - 1
    )
    padded = np.full((SLOT, SLOT), -1)
    padded[:CELLS, :CELLS] = rel
    return jnp.asarray(padded.reshape(-1), jnp.int32)[:, None] == jnp.arange(side * side)[None, :]


def shift_matrix():
    cell = np.arange(SIDE * SIDE).reshape(SIDE, SIDE)

    def slots(grid):
        blocks = grid.reshape(SIDE // WIN, WIN, SIDE // WIN, WIN).swapaxes(1, 2)
        blocks = blocks.reshape(WINDOWS, CELLS)
        return np.pad(blocks, ((0, 0), (0, SLOT - CELLS)), constant_values=-1).reshape(-1)

    plain, moved = slots(cell), slots(np.roll(cell, (-SHIFT, -SHIFT), axis=(0, 1)))
    plain = np.where(plain < 0, -2, plain)
    return low(jnp.asarray(moved, jnp.int32)[:, None] == jnp.asarray(plain, jnp.int32)[None, :])


def to_slots(grid):
    blocks = to_windows(grid)
    return jnp.pad(blocks, ((0, 0), (0, SLOT - CELLS), (0, 0))).reshape(TOKENS, grid.shape[3])


def from_slots(rows):
    return from_windows(rows.reshape(WINDOWS, SLOT, -1)[:, :CELLS], 1)


def body(
    images, cotangent, regions, w_qkv, w_proj, w_fc1, w_fc2,
    norm_gains, norm_shifts, branch_biases, fc1_bias, rel_table,
    rep_count, shard_count,
):
    layer_count = w_qkv.shape[0]
    width = w_proj.shape[2]
    head_count = rel_table.shape[2]
    head_dim = width // head_count
    hidden = w_fc1.shape[2]
    rows, hidden_own = w_qkv.shape[1], w_fc2.shape[1]
    gathered = []
    for n in range(layer_count):
        own = pack_local(
            w_qkv[n], w_proj[n], w_fc1[n], w_fc2[n],
            norm_gains[n], norm_shifts[n], branch_biases[n], fc1_bias[n],
        )
        gathered.append(lax.all_gather(own, "shard", axis=0, tiled=False))
    onehot = table_onehot()
    spare = jnp.where(jnp.arange(SLOT) < CELLS, 0.0, -1e30).astype(jnp.float32)
    score_bias = lax.dot_general(
        rel_table, low(onehot), (((1,), (1,)), ((), ())), preferred_element_type=jnp.float32
    )
    score_bias = score_bias.reshape(layer_count, head_count * SLOT, SLOT) + spare
    region_win = jnp.pad(to_windows(regions), ((0, 0), (0, SLOT - CELLS)), constant_values=-1)
    region_mask = jnp.where(region_win[:, :, None] == region_win[:, None, :], 0.0, -100.0).astype(
        jnp.float32
    )
    perm = shift_matrix()
    f32, bf16 = jnp.float32, jnp.bfloat16
    residual = to_slots(images).astype(f32)
    flops = 2 * TOKENS * (4 * width + 2 * hidden) * width
    saved = []
    for n in range(layer_count):
        shifted = n % 2 == 1
        packed = gathered[n]
        small = packed[:, packed.shape[1] - PAD_ROWS]
        vec = small[:, : 8 * rows].reshape(shard_count, 8, rows)
        vec = jnp.swapaxes(vec, 0, 1).reshape(8, width).astype(f32)
        fb = small[:, 8 * rows : 8 * rows + hidden_own].reshape(1, hidden).astype(f32)
        extra = [region_mask, perm] if shifted else []
        out, *acts = call_kernel(
            functools.partial(forward_kernel, shifted, hidden, head_dim),
            [
                ((TOKENS, width), f32), ((TOKENS, width), bf16), ((TOKENS, 3 * width), bf16),
                ((TOKENS, width), bf16), ((TOKENS, width), f32), ((TOKENS, width), bf16),
                ((TOKENS, hidden), f32), ((TOKENS, hidden), bf16),
            ],
            [],
            [residual, packed, vec, fb, score_bias[n], *extra],
            flops,
            "block_forward",
        )
        saved.append((packed, vec, extra, [residual, *acts]))
        residual = out
    images_out = from_slots(low(residual))
    upstream = to_slots(cotangent).astype(f32)
    shares = [None] * layer_count
    tables = [None] * layer_count
    for n in reversed(range(layer_count)):
        packed, vec, extra, acts = saved[n]
        upstream, weight_grads, small, tables[n] = call_kernel(
            functools.partial(backward_kernel, n % 2 == 1, hidden, head_dim),
            [
                ((TOKENS, width), f32), (packed.shape, bf16),
                ((8 + hidden // width + 4, width), f32), ((head_count * SLOT, SLOT), f32),
            ],
            [((TOKENS, width), bf16), ((TOKENS, 3 * width), bf16)],
            [upstream, packed, vec, score_bias[n], *extra, *acts],
            2 * flops,
            "block_backward",
        )
        vec_part = jnp.swapaxes(small[:8].reshape(8, shard_count, rows), 0, 1)
        fb_part = small[8 : 8 + hidden // width].reshape(shard_count, hidden_own)
        small = low(jnp.concatenate([vec_part.reshape(shard_count, -1), fb_part], axis=1))
        weight_grads = lax.dynamic_update_slice(
            weight_grads, small[:, None], (0, packed.shape[1] - PAD_ROWS, 0)
        )
        shares[n] = lax.psum_scatter(weight_grads, "shard", scatter_dimension=0, tiled=False)
    summed = unpack_shares(rep_sum(jnp.stack(shares), rep_count), w_qkv, w_fc2, fc1_bias)
    table_terms = jnp.stack(tables).reshape(layer_count, head_count, SLOT * SLOT)
    table_grad = lax.dot_general(
        onehot.astype(f32), table_terms, (((0,), (2,)), ((), ())), precision=highest
    )
    table_total = lax.psum(jnp.swapaxes(table_grad, 0, 1), ("rep", "shard"))
    return (images_out, from_slots(upstream), *summed, table_total)


def solution(mesh):
    return jax.shard_map(
        functools.partial(
            body, rep_count=mesh.shape["rep"], shard_count=mesh.shape["shard"]
        ),
        mesh=mesh,
        in_specs=(
            P(("rep", "shard"), None, None, None),
            P(("rep", "shard"), None, None, None),
            P(("rep", "shard"), None, None),
            P(None, "shard", None),
            P(None, "shard", None),
            P(None, "shard", None),
            P(None, "shard", None),
            P(None, None, "shard"),
            P(None, None, "shard"),
            P(None, None, "shard"),
            P(None, "shard"),
            P(),
        ),
        out_specs=(
            P(("rep", "shard"), None, None, None),
            P(("rep", "shard"), None, None, None),
            P(None, "shard", None),
            P(None, "shard", None),
            P(None, "shard", None),
            P(None, "shard", None),
            P(None, None, "shard"),
            P(None, None, "shard"),
            P(None, None, "shard"),
            P(None, "shard"),
            P(),
        ),
        check_vma=False,
    )
```

time: 647 us -> 460 us (0.71)
  local copies, waits for them, and re-layouts: 152 us -> 30.3 us
  matrix products: 74.3 us -> 2.15 us
  Pallas kernels: 0 us -> 65.4 us
  other arithmetic: 67.1 us -> 7.22 us
  waiting for transfers between devices: 279 us -> 294 us
    dot_general x42 -> x1, matrix products: 74.3 us -> 1.55 us  [body(): lax.dot_general(onehot.astype(f32), table_terms, (((0,), (2,)), ((), ()))...]
    pallas_call x0 -> x4, Pallas kernels: none -> 65.4 us  [call_kernel(): pl.pallas_call(kernel, out_shape=[jax.ShapeDtypeStruct(shape, kind) for s...]
    reduce_sum x28 -> x0, other arithmetic: 50.5 us -> none  [the longest x6 17 us: layer_norm(): return centred * lax.rsqrt(row_var + eps) * norm_gain + norm_shift]
    reshape x38 -> x15, local copies, waits for them, and re-layouts: 49.3 us -> 2.27 us  [the longest x1 0.74 us: from_windows(): return grid_data.reshape((image_count, SIDE, SIDE) + trailing)]
    unnamed x290 -> x43, local copies, waits for them, and re-layouts: 30.6 us -> 5.13 us
    slice x29 -> x11, local copies, waits for them, and re-layouts: 21 us -> 4.98 us  [the longest x2 1.85 us: body(): small = packed[:, packed.shape[1] - PAD_ROWS]]
    convert_element_type x17 -> x6, local copies, waits for them, and re-layouts: 17.3 us -> 1.55 us  [body(): vec = jnp.swapaxes(vec, 0, 1).reshape(8, width).astype(f32)]
    reduce_scatter x2, waiting for transfers between devices: 157 us -> 172 us  [body(): lax.psum_scatter(weight_grads, 'shard', scatter_dimension=0, tiled=False)]
  transfers between devices with their start and end apart: 5 -> 5, of which waited for: 4 -> 4; matrix products, arithmetic and copies ran while one was open for 5% -> 4% of each run, Pallas kernels for 0% -> 0%
where the time goes in v2:
time: 460 us; the launch traced here: 459 us
  waiting for transfers between devices  294 us (64%)
  Pallas kernels  65.4 us (14%)
  blocking collectives  44.3 us (10%)
  local copies, waits for them, and re-layouts  30.3 us (7%)
  between operations  14.3 us (3%)
  other arithmetic  7.22 us (2%)
    reduce_scatter x2, waiting for transfers between devices, body(): lax.psum_scatter(weight_grads, 'shard', scatter_dimension=0, tiled=False)  172 us
    all_gather x2, waiting for transfers between devices, body(): gathered.append(lax.all_gather(own, 'shard', axis=0, tiled=False))  122 us
    pallas_call x4, Pallas kernels, call_kernel(): pl.pallas_call(kernel, out_shape=[jax.ShapeDtypeStruct(shape, kind) for s...  65.4 us
    psum x1, blocking collectives, body(): table_total = lax.psum(jnp.swapaxes(table_grad, 0, 1), ('rep', 'shard'))  44.3 us
  transfers between devices with their start and end apart: 5, of which 4 were waited for; matrix products, arithmetic and copies ran while one was open for 4% of the time, Pallas kernels for 0%

profile of v2, /device:TPU:0, one launch (start us, length us, event | category | flops | bytes accessed | tf_op | source)
XLA Modules:
  0.0 459.4 jit_solution(10468932187423404886)
XLA Ops:
  7.3 1.0 slice_bitcast_fusion.4
  8.3 1.0 slice_bitcast_fusion.2
  13.6 1.0 bitcast_dynamic-update-slice_fusion
  21.4 1.0 slice_bitcast_fusion
  22.4 59.2 %all-gather.5.cloned.1.call-done = bf16[6400,512]{1,0:T(8,128)(2,1)} async-done(((bf16[400,512]{1,0:T(8,128)(2,1)}), bf16[6400,512]{1,0:T(8,128)(2,1)}) %all-gather.5.cloned.1.call-update) | async-done | bytes 6553616 | tf_op jit(solution)/shard_map/all_gather | solution.py:403
  81.7 0.9 slice.245
  83.2 62.7 %all-gather.7.cloned.1.call-done = bf16[6400,512]{1,0:T(8,128)(2,1)} async-done(((bf16[400,512]{1,0:T(8,128)(2,1)}), bf16[6400,512]{1,0:T(8,128)(2,1)}) %all-gather.7.cloned.1.call-update) | async-done | bytes 6553616 | tf_op jit(solution)/shard_map/all_gather | solution.py:403
  145.9 0.9 slice.256
  149.0 11.7 %block_forward.2 = (f32[256,512]{1,0:T(8,128)}, bf16[256,512]{1,0:T(8,128)(2,1)}, bf16[256,1536]{1,0:T(8,128)(2,1)}, bf16[256,512]{1,0:T(8,128)(2,1)}, f32[256,5...) custom-call(f32[256,512]{1,0:T(8,128)} %bitcast_convert_fusion.1.refs_0_.refs_4_, ...), custom_call_target="tpu_custom_call" | custom-call | flops 1610612736 | bytes 20000000 | tf_op jit(solution)/shard_map/block_forward/pallas_call | solution.py:340
  160.7 11.8 %block_forward.3 = (f32[256,512]{1,0:T(8,128)}, bf16[256,512]{1,0:T(8,128)(2,1)}, bf16[256,1536]{1,0:T(8,128)(2,1)}, bf16[256,512]{1,0:T(8,128)(2,1)}, f32[256,5...) custom-call(f32[256,512]{1,0:T(8,128)} %get-tuple-element.35.refs_0_.refs_6_, ...), custom_call_target="tpu_custom_call" | custom-call | flops 1610612736 | bytes 20000000 | tf_op jit(solution)/shard_map/block_forward/pallas_call | solution.py:340
  172.5 21.3 %block_backward.2 = (f32[256,512]{1,0:T(8,128)}, bf16[16,400,512]{2,1,0:T(8,128)(2,1)}, f32[16,512]{1,0:T(8,128)}, f32[1024,64]{1,0:T(8,128)}) custom-call(f32[256,512]{1,0:T(8,128)} %bitcast_convert_fusion.refs_0_, bf16[16,400,512]{2,1,0:T(8,128)(2,1)} %bitcast.89, f32[8,512]{1,0:T(8,128)} %reshape.240.refs_2_, ...), custom_call_target="tpu_custom_call" | custom-call | flops 3221225472 | bytes 20000000 | tf_op jit(solution)/shard_map/block_backward/pallas_call | solution.py:340
  193.9 20.5 %block_backward.3 = (f32[256,512]{1,0:T(8,128)}, bf16[16,400,512]{2,1,0:T(8,128)(2,1)}, f32[16,512]{1,0:T(8,128)}, f32[1024,64]{1,0:T(8,128)}) custom-call(f32[256,512]{1,0:T(8,128)} %get-tuple-element.44.refs_0_, bf16[16,400,512]{2,1,0:T(8,128)(2,1)} %bitcast.86, f32[8,512]{1,0:T(8,128)} %reshape.238.refs_2_, f32[1024,64]{1,0:T(8,128)} %get-tuple-element.68.refs_4_.refs_3_, ...), custom_call_target="tpu_custom_call" | custom-call | flops 3221225472 | bytes 20000000 | tf_op jit(solution)/shard_map/block_backward/pallas_call | solution.py:340
  215.5 1.9 dynamic_update_slice.6
  218.4 1.9 dynamic_update_slice.7
  220.3 82.8 %reduce-scatter.3.cloned.1.call-done = bf16[1,400,512]{2,1,0:T(8,128)(2,1)} async-done(((bf16[16,400,512]{2,1,0:T(8,128)(2,1)}), bf16[1,400,512]{2,1,0:T(8,128)(2,1)}) %reduce-scatter.3.cloned.1.call-update) | async-done | bytes 409616 | tf_op jit(solution)/shard_map/reduce_scatter | solution.py:464
  303.0 1.0 constant_dynamic-update-slice_fusion.19
  304.0 89.3 %reduce-scatter.5.cloned.1.call-done = bf16[1,400,512]{2,1,0:T(8,128)(2,1)} async-done(((bf16[16,400,512]{2,1,0:T(8,128)(2,1)}), bf16[1,400,512]{2,1,0:T(8,128)(2,1)}) %reduce-scatter.5.cloned.1.call-update) | async-done | bytes 409616 | tf_op jit(solution)/shard_map/reduce_scatter | solution.py:464
  393.4 1.0 constant_dynamic-update-slice_fusion.18
  394.4 1.5 collective-permute-start
  397.0 1.0 slice.261
  398.5 1.2 copy.79
  399.8 1.2 stack.13
  401.1 1.6 fusion.6
  402.6 44.3 %psum.7 = f32[2,169,16]{1,2,0:T(8,128)} all-reduce(f32[2,169,16]{1,2,0:T(8,128)S(1)} %fusion.6), channel_id=1, replica_groups=mesh['rep'=2,'shard'=16] {'rep','shard'}, use_global_device_ids=true, to_apply=%region_2.3 | all-reduce | flops 5408 | bytes 43264 | tf_op jit(solution)/shard_map/psum | solution.py:470
  (132 shorter events, 23.2 us)
Async XLA Ops:
  7.2 9.4 %copy-start = (bf16[2,169,16]{1,2,0:T(8,128)(2,1)S(1)}, bf16[2,169,16]{1,2,0:T(8,128)(2,1)}, u32[]{:S(2)}) copy-start(bf16[2,169,16]{1,2,0:T(8,128)(2,1)} %param.26) | copy-start | bytes 32452
  7.2 9.4 %copy-start.11 = (s32[4096]{0:T(1024)S(1)}, s32[4096]{0:T(1024)}, u32[]{:S(2)}) copy-start(s32[4096]{0:T(1024)} %constant.22.clone) | copy-start | bytes 49156
  7.2 9.1 %copy-start.5 = (bf16[1,14,14,512]{3,2,1,0:T(8,128)(2,1)S(1)}, bf16[1,14,14,512]{3,2,1,0:T(8,128)(2,1)}, u32[]{:S(2)}) copy-start(bf16[1,14,14,512]{3,2,1,0:T(8,128)(2,1)} %param.15) | copy-start | bytes 602116
  7.2 74.4 %all-gather.5.cloned.1.call-start = ((), (), s32[]{:S(2)}) async-start(), calls=%async_computation.4 | async-start | bytes 6963200 | tf_op jit(solution)/shard_map/all_gather | solution.py:403
  10.1 7.5 %copy-start.8 = (s32[1,14,14]{2,0,1:T(1,128)S(1)}, s32[1,14,14]{2,0,1:T(1,128)}, u32[]{:S(2)}) copy-start(s32[1,14,14]{2,0,1:T(1,128)} %param.17) | copy-start | bytes 2356
  10.1 7.7 %copy-start.6 = (bf16[1,14,14,512]{3,2,1,0:T(8,128)(2,1)S(1)}, bf16[1,14,14,512]{3,2,1,0:T(8,128)(2,1)}, u32[]{:S(2)}) copy-start(bf16[1,14,14,512]{3,2,1,0:T(8,128)(2,1)} %param.16) | copy-start | bytes 602116
  14.6 0.8 copy-start.3
  15.4 130.5 %all-gather.7.cloned.1.call-start = ((), (), s32[]{:S(2)}) async-start(), calls=%async_computation.5 | async-start | bytes 6963200 | tf_op jit(solution)/shard_map/all_gather | solution.py:403
  15.5 0.8 copy-start.4
  16.3 286.7 %reduce-scatter.3.cloned.1.call-start = ((), (), s32[]{:S(2)}) async-start(), calls=%async_computation.2 | async-start | bytes 6963200 | tf_op jit(solution)/shard_map/reduce_scatter | solution.py:464
  16.4 1.6 copy-start.9
  16.4 1.6 copy-start.10
  217.3 0.8 copy-start.7
  217.4 176.0 %reduce-scatter.5.cloned.1.call-start = ((), (), s32[]{:S(2)}) async-start(), calls=%async_computation.3 | async-start | bytes 6963200 | tf_op jit(solution)/shard_map/reduce_scatter | solution.py:464
  220.2 175.7 %copy-start.2 = (f32[256,512]{1,0:T(8,128)S(1)}, f32[256,512]{1,0:T(8,128)}, u32[]{:S(2)}) copy-start(f32[256,512]{1,0:T(8,128)} %get-tuple-element.36) | copy-start | bytes 1572868
  394.4 52.6 %collective-permute-start = (bf16[2,400,512]{2,1,0:T(8,128)(2,1)S(1)}, bf16[2,400,512]{2,1,0:T(8,128)(2,1)S(1)}, u32[]{:S(2)}, u32[]{:S(2)}) collective-permute-start(bf16[2,400,512]{2,1,0:T(8,128)(2,1)S(1)} %constant_dynamic-update-slice_fusion.18), channel_id=1, source_target_pairs={{0,16},{16,0},{1,17},{17,1},{2,18},{18,2},{3,19},{19,3},{4,20},{20... | collective-permute-start | bytes 2457608 | tf_op jit(solution)/shard_map/ppermute | solution.py:63
  395.9 3.7 copy-start.1
Sparse Core Ops, SparseCore 0:
  15.5 66.0 all-gather.4
  83.9 61.9 all-gather.6
  217.5 85.4 reduce-scatter.2
  307.3 85.9 reduce-scatter.4

commit v3 on v2

--- a/solution.py
+++ b/solution.py
@@ -41,52 +41,57 @@
     return grid_data.reshape((image_count, SIDE, SIDE) + trailing)
 
 
+def vector_tile(parts, width):
+    parts = [jnp.pad(part, ((0, width - part.shape[0]),)) for part in parts]
+    return jnp.pad(jnp.stack(parts), ((0, PAD_ROWS - len(parts)), (0, 0)))
+
+
 def pack_local(w_qkv, w_proj, w_fc1, w_fc2, gains, shifts, biases, fc1_bias):
-    width = w_proj.shape[1]
-    blocks = [w_qkv[:, n * width : (n + 1) * width] for n in range(w_qkv.shape[1] // width)]
-    blocks.append(w_proj)
-    blocks += [w_fc1[:, n * width : (n + 1) * width] for n in range(w_fc1.shape[1] // width)]
-    blocks.append(w_fc2)
-    small = jnp.concatenate(
-        [gains.reshape(-1), shifts.reshape(-1), biases.reshape(-1), fc1_bias.reshape(-1)]
-    )
-    small = jnp.pad(small, (0, width - small.shape[0])).reshape(1, width)
-    blocks.append(jnp.pad(small, ((0, PAD_ROWS - 1), (0, 0))))
-    return jnp.concatenate(blocks, axis=0)
+    width = w_proj.shape[2]
+    blocks, smalls = [], []
+    for n in range(w_qkv.shape[0]):
+        for block in (w_qkv[n], w_proj[n], w_fc1[n], w_fc2[n]):
+            parts = block.shape[1] // width
+            blocks += [block[:, m * width : (m + 1) * width] for m in range(parts)]
+        vectors = (gains[n], shifts[n], biases[n], fc1_bias[n])
+        smalls.append(jnp.concatenate([vector.reshape(-1) for vector in vectors]))
+    return jnp.concatenate([*blocks, vector_tile(smalls, width)], axis=0)
 
 
 def rep_sum(share, rep_count):
-    total = share
+    total = share.astype(jnp.float32)
     step = 1
     while step < rep_count:
         pairs = [(n, n ^ step) for n in range(rep_count)]
-        total = total + lax.ppermute(total, "rep", pairs)
+        sent = low(total)
+        arrived = lax.ppermute(sent, "rep", pairs)
+        total = sent.astype(jnp.float32) + arrived.astype(jnp.float32)
         step *= 2
     return total
 
 
 def unpack_shares(shares, w_qkv, w_fc2, fc1_bias):
-    shares = shares.astype(jnp.float32)
-    layer_count, _, width = shares.shape
-    rows = w_qkv.shape[1]
-    hidden = fc1_bias.shape[1]
+    layer_count, rows = w_qkv.shape[:2]
+    width = shares.shape[1]
+    hidden_own = fc1_bias.shape[1]
+    blocks = shares[:-PAD_ROWS].reshape(layer_count, -1, width)
     qkv_parts = w_qkv.shape[2] // width
-    fc1_parts = (shares.shape[1] - PAD_ROWS - w_fc2.shape[1]) // rows - qkv_parts - 1
+    fc1_parts = (blocks.shape[1] - w_fc2.shape[1]) // rows - qkv_parts - 1
 
     def piece(n):
-        return shares[:, n * rows : (n + 1) * rows]
+        return blocks[:, n * rows : (n + 1) * rows]
 
     start = (qkv_parts + 1 + fc1_parts) * rows
-    small = shares[:, start + w_fc2.shape[1]]
+    small = shares[blocks.shape[0] * blocks.shape[1] :][:layer_count]
     return (
         jnp.concatenate([piece(n) for n in range(qkv_parts)], axis=2),
         piece(qkv_parts),
         jnp.concatenate([piece(qkv_parts + 1 + n) for n in range(fc1_parts)], axis=2),
-        shares[:, start : start + w_fc2.shape[1]],
+        blocks[:, start:],
         small[:, : 2 * rows].reshape(layer_count, 2, rows),
         small[:, 2 * rows : 4 * rows].reshape(layer_count, 2, rows),
         small[:, 4 * rows : 8 * rows].reshape(layer_count, 4, rows),
-        small[:, 8 * rows : 8 * rows + hidden],
+        small[:, 8 * rows : 8 * rows + hidden_own],
     )
 
 
@@ -127,17 +132,22 @@
 
 
 class Pieces:
-    def __init__(self, ref, width, hidden):
+    def __init__(self, ref, width, hidden, layer):
         self.ref = ref
         self.width = width
         self.shards = ref.shape[0]
         self.rows = width // self.shards
         self.hidden = hidden // self.shards
         self.parts = hidden // width
-        self.start = (4 + self.parts) * self.rows
+        self.base = layer * ((4 + self.parts) * self.rows + self.hidden)
+        self.start = self.base + (4 + self.parts) * self.rows
+
+    def span(self, n):
+        first = self.base + n * self.rows
+        return slice(first, first + self.rows)
 
     def square(self, n):
-        return self.ref[:, n * self.rows : (n + 1) * self.rows, :].reshape(self.width, self.width)
+        return self.ref[:, self.span(n), :].reshape(self.width, self.width)
 
     def second(self, n):
         group = self.shards // self.parts
@@ -146,7 +156,7 @@
         ].reshape(self.width, self.width)
 
     def put_square(self, n, value):
-        self.ref[:, n * self.rows : (n + 1) * self.rows, :] = low(value).reshape(
+        self.ref[:, self.span(n), :] = low(value).reshape(
             self.shards, self.rows, self.width
         )
 
@@ -186,15 +196,16 @@
     return raised / jnp.sum(raised, axis=-1, keepdims=True)
 
 
-def forward_kernel(shifted, hidden, head_dim, *refs):
-    if shifted:
-        (r_ref, w_ref, vec_ref, fb_ref, bias_ref, mask_ref, perm_ref, *outs) = refs
-    else:
-        (r_ref, w_ref, vec_ref, fb_ref, bias_ref, *outs) = refs
-        mask_ref = None
-    (out_ref, hs_ref, qkv_ref, mixed_ref, mid_ref, h2_ref, slope_ref, act_ref) = outs
+def forward_block(layer, hidden, head_dim, r_ref, out_ref, ins, acts):
+    shifted = layer % 2 == 1
+    (w_ref, vec_ref, fb_ref, bias_ref, mask_ref, perm_ref) = ins
+    vec_ref, fb_ref, bias_ref = vec_ref.at[layer], fb_ref.at[layer], bias_ref.at[layer]
+    mask_ref = mask_ref if shifted else None
+    (hs_ref, qkv_ref, mixed_ref, mid_ref, h2_ref, slope_ref, act_ref) = (
+        act.at[layer] for act in acts
+    )
     width = r_ref.shape[1]
-    weights = Pieces(w_ref, width, hidden)
+    weights = Pieces(w_ref, width, hidden, layer)
     scale = head_dim ** (-0.5)
     per_group = LANES // head_dim
     vec = lambda n: vec_ref[n : n + 1, :]
@@ -242,17 +253,19 @@
         out_ref[...] += dot(act, weights.second(part))
 
 
-def backward_kernel(shifted, hidden, head_dim, *refs):
-    if shifted:
-        (g_ref, w_ref, vec_ref, bias_ref, mask_ref, perm_ref, *rest) = refs
-    else:
-        (g_ref, w_ref, vec_ref, bias_ref, *rest) = refs
-        mask_ref = None
-    (r_ref, hs_ref, qkv_ref, mixed_ref, mid_ref, h2_ref, slope_ref, act_ref, *rest) = rest
-    (up_ref, gw_ref, small_ref, ds_ref, dmix_ref, dqkv_ref) = rest
+def backward_block(layer, hidden, head_dim, r_ref, g_ref, up_ref, ins, acts, gw_ref, rest):
+    shifted = layer % 2 == 1
+    (w_ref, vec_ref, _, bias_ref, mask_ref, perm_ref) = ins
+    vec_ref, bias_ref = vec_ref.at[layer], bias_ref.at[layer]
+    mask_ref = mask_ref if shifted else None
+    (hs_ref, qkv_ref, mixed_ref, mid_ref, h2_ref, slope_ref, act_ref) = (
+        act.at[layer] for act in acts
+    )
+    (small_ref, ds_ref, dmix_ref, dqkv_ref) = rest
+    small_ref, ds_ref = small_ref.at[layer], ds_ref.at[layer]
     width = r_ref.shape[1]
-    weights = Pieces(w_ref, width, hidden)
-    grads = Pieces(gw_ref, width, hidden)
+    weights = Pieces(w_ref, width, hidden, layer)
+    grads = Pieces(gw_ref, width, hidden, layer)
     scale = head_dim ** (-0.5)
     per_group = LANES // head_dim
     vec = lambda n: vec_ref[n : n + 1, :]
@@ -261,10 +274,6 @@
         small_ref[n : n + 1, :] = jnp.sum(values.astype(jnp.float32), axis=0, keepdims=True)
 
     small_ref[...] = jnp.zeros_like(small_ref)
-    first_spare = grads.start + grads.hidden
-    gw_ref[:, first_spare:, :] = jnp.zeros(
-        (grads.shards, gw_ref.shape[1] - first_spare, width), jnp.bfloat16
-    )
     upstream = g_ref[...]
     out_grad = low(upstream)
     put_sum(7, out_grad)
@@ -335,6 +344,28 @@
     up_ref[...] = middle_grad + norm_back(rows_grad, vec(0), xhat, rstd)
 
 
+def step_kernel(layer_count, hidden, head_dim, *refs):
+    (x_ref, ct_ref, *ins) = refs[:8]
+    (out_ref, up_ref, gw_ref, small_ref, ds_ref) = refs[8:13]
+    (res_ref, grad_ref, *acts, dmix_ref, dqkv_ref) = refs[13:]
+    res_ref[0] = x_ref[...].astype(jnp.float32)
+    for layer in range(layer_count):
+        forward_block(
+            layer, hidden, head_dim, res_ref.at[layer], res_ref.at[layer + 1], ins, acts
+        )
+    out_ref[...] = low(res_ref[layer_count])
+    grad_ref[...] = ct_ref[...].astype(jnp.float32)
+    gw_ref[:, gw_ref.shape[1] - PAD_ROWS :, :] = jnp.zeros(
+        (gw_ref.shape[0], PAD_ROWS, gw_ref.shape[2]), jnp.bfloat16
+    )
+    rest = (small_ref, ds_ref, dmix_ref, dqkv_ref)
+    for layer in reversed(range(layer_count)):
+        target = grad_ref if layer else up_ref
+        backward_block(
+            layer, hidden, head_dim, res_ref.at[layer], grad_ref, target, ins, acts, gw_ref, rest
+        )
+
+
 def call_kernel(kernel, outs, scratch, args, flops, name):
     vmem = pl.BlockSpec(memory_space=pltpu.VMEM)
     return pl.pallas_call(
@@ -394,13 +425,10 @@
     head_dim = width // head_count
     hidden = w_fc1.shape[2]
     rows, hidden_own = w_qkv.shape[1], w_fc2.shape[1]
-    gathered = []
-    for n in range(layer_count):
-        own = pack_local(
-            w_qkv[n], w_proj[n], w_fc1[n], w_fc2[n],
-            norm_gains[n], norm_shifts[n], branch_biases[n], fc1_bias[n],
-        )
-        gathered.append(lax.all_gather(own, "shard", axis=0, tiled=False))
+    own = pack_local(
+        w_qkv, w_proj, w_fc1, w_fc2, norm_gains, norm_shifts, branch_biases, fc1_bias
+    )
+    packed = lax.all_gather(own, "shard", axis=0, tiled=False)
     onehot = table_onehot()
     spare = jnp.where(jnp.arange(SLOT) < CELLS, 0.0, -1e30).astype(jnp.float32)
     score_bias = lax.dot_general(
@@ -413,62 +441,68 @@
     )
     perm = shift_matrix()
     f32, bf16 = jnp.float32, jnp.bfloat16
-    residual = to_slots(images).astype(f32)
-    flops = 2 * TOKENS * (4 * width + 2 * hidden) * width
-    saved = []
-    for n in range(layer_count):
-        shifted = n % 2 == 1
-        packed = gathered[n]
-        small = packed[:, packed.shape[1] - PAD_ROWS]
-        vec = small[:, : 8 * rows].reshape(shard_count, 8, rows)
-        vec = jnp.swapaxes(vec, 0, 1).reshape(8, width).astype(f32)
-        fb = small[:, 8 * rows : 8 * rows + hidden_own].reshape(1, hidden).astype(f32)
-        extra = [region_mask, perm] if shifted else []
-        out, *acts = call_kernel(
-            functools.partial(forward_kernel, shifted, hidden, head_dim),
-            [
-                ((TOKENS, width), f32), ((TOKENS, width), bf16), ((TOKENS, 3 * width), bf16),
-                ((TOKENS, width), bf16), ((TOKENS, width), f32), ((TOKENS, width), bf16),
-                ((TOKENS, hidden), f32), ((TOKENS, hidden), bf16),
-            ],
-            [],
-            [residual, packed, vec, fb, score_bias[n], *extra],
-            flops,
-            "block_forward",
-        )
-        saved.append((packed, vec, extra, [residual, *acts]))
-        residual = out
-    images_out = from_slots(low(residual))
-    upstream = to_slots(cotangent).astype(f32)
-    shares = [None] * layer_count
-    tables = [None] * layer_count
-    for n in reversed(range(layer_count)):
-        packed, vec, extra, acts = saved[n]
-        upstream, weight_grads, small, tables[n] = call_kernel(
-            functools.partial(backward_kernel, n % 2 == 1, hidden, head_dim),
-            [
-                ((TOKENS, width), f32), (packed.shape, bf16),
-                ((8 + hidden // width + 4, width), f32), ((head_count * SLOT, SLOT), f32),
-            ],
-            [((TOKENS, width), bf16), ((TOKENS, 3 * width), bf16)],
-            [upstream, packed, vec, score_bias[n], *extra, *acts],
-            2 * flops,
-            "block_backward",
-        )
-        vec_part = jnp.swapaxes(small[:8].reshape(8, shard_count, rows), 0, 1)
-        fb_part = small[8 : 8 + hidden // width].reshape(shard_count, hidden_own)
-        small = low(jnp.concatenate([vec_part.reshape(shard_count, -1), fb_part], axis=1))
-        weight_grads = lax.dynamic_update_slice(
-            weight_grads, small[:, None], (0, packed.shape[1] - PAD_ROWS, 0)
-        )
-        shares[n] = lax.psum_scatter(weight_grads, "shard", scatter_dimension=0, tiled=False)
-    summed = unpack_shares(rep_sum(jnp.stack(shares), rep_count), w_qkv, w_fc2, fc1_bias)
-    table_terms = jnp.stack(tables).reshape(layer_count, head_count, SLOT * SLOT)
+    flops = 6 * layer_count * TOKENS * (4 * width + 2 * hidden) * width
+    small = packed[:, packed.shape[1] - PAD_ROWS :][:, :layer_count]
+    vec = small[:, :, : 8 * rows].reshape(shard_count, layer_count, 8, rows)
+    vec = vec.transpose(1, 2, 0, 3).reshape(layer_count, 8, width).astype(f32)
+    fb = small[:, :, 8 * rows : 8 * rows + hidden_own]
+    fb = jnp.swapaxes(fb, 0, 1).reshape(layer_count, 1, hidden).astype(f32)
+
+    def kept(columns, kind):
+        return ((layer_count, TOKENS, columns), kind)
+
+    out, upstream, weight_grads, small, tables = call_kernel(
+        functools.partial(step_kernel, layer_count, hidden, head_dim),
+        [
+            ((TOKENS, width), bf16), ((TOKENS, width), f32), (packed.shape, bf16),
+            ((layer_count, 8 + hidden // width + 4, width), f32),
+            ((layer_count, head_count * SLOT, SLOT), f32),
+        ],
+        [
+            ((layer_count + 1, TOKENS, width), f32), ((TOKENS, width), f32),
+            kept(width, bf16), kept(3 * width, bf16), kept(width, bf16), kept(width, f32),
+            kept(width, bf16), kept(hidden, f32), kept(hidden, bf16),
+            ((TOKENS, width), bf16), ((TOKENS, 3 * width), bf16),
+        ],
+        [to_slots(images), to_slots(cotangent), packed, vec, fb, score_bias, region_mask, perm],
+        flops,
+        "both_blocks",
+    )
+    vec_part = small[:, :8].reshape(layer_count, 8, shard_count, rows).transpose(2, 0, 1, 3)
+    vec_part = vec_part.reshape(shard_count, layer_count, 8 * rows)
+    fb_part = small[:, 8 : 8 + hidden // width].reshape(layer_count, shard_count, hidden_own)
+    small = jnp.concatenate([vec_part, jnp.swapaxes(fb_part, 0, 1)], axis=2)
+    entries = rel_table.shape[1]
+    entries_own = -(-entries // shard_count)
+    table_terms = tables.reshape(layer_count, head_count, SLOT * SLOT)
     table_grad = lax.dot_general(
         onehot.astype(f32), table_terms, (((0,), (2,)), ((), ())), precision=highest
     )
-    table_total = lax.psum(jnp.swapaxes(table_grad, 0, 1), ("rep", "shard"))
-    return (images_out, from_slots(upstream), *summed, table_total)
+    table_grad = jnp.pad(table_grad, ((0, entries_own * shard_count - entries), (0, 0), (0, 0)))
+    table_grad = table_grad.reshape(shard_count, entries_own, layer_count, head_count)
+    table_grad = jnp.swapaxes(table_grad, 1, 2).reshape(shard_count, layer_count, -1)
+
+    def widen(part):
+        return jnp.pad(low(part), ((0, 0), (0, 0), (0, width - part.shape[2])))
+
+    tail = jnp.concatenate([widen(small), widen(table_grad)], axis=1)
+    tail = jnp.pad(tail, ((0, 0), (0, PAD_ROWS - tail.shape[1]), (0, 0)))
+    weight_grads = lax.dynamic_update_slice(
+        weight_grads, tail, (0, packed.shape[1] - PAD_ROWS, 0)
+    )
+    share = lax.psum_scatter(weight_grads, "shard", scatter_dimension=0, tiled=False)
+    total = rep_sum(share, rep_count)
+    first = total.shape[0] - PAD_ROWS + layer_count
+    table_own = total[first : first + layer_count, : entries_own * head_count]
+    table_all = lax.all_gather(table_own, "shard", axis=0, tiled=False)
+    table_all = table_all.reshape(shard_count, layer_count, entries_own, head_count)
+    table_total = jnp.swapaxes(table_all, 0, 1).reshape(layer_count, -1, head_count)
+    return (
+        from_slots(out),
+        from_slots(upstream),
+        *unpack_shares(total, w_qkv, w_fc2, fc1_bias),
+        table_total[:, :entries],
+    )
 
 
 def solution(mesh):

time: 460 us -> 372 us (0.81)
  waiting for transfers between devices: 294 us -> 249 us
  blocking collectives: 44.3 us -> 20.6 us
  Pallas kernels: 65.4 us -> 51.1 us
  local copies, waits for them, and re-layouts: 30.3 us -> 24.6 us
    psum x1 -> x0, blocking collectives: 44.3 us -> none  [body(): table_total = lax.psum(jnp.swapaxes(table_grad, 0, 1), ('rep', 'shard'))]
    reduce_scatter x2 -> x1, waiting for transfers between devices: 172 us -> 135 us  [body(): lax.psum_scatter(weight_grads, 'shard', scatter_dimension=0, tiled=False)]
    all_gather x2 -> x1, waiting for transfers between devices: 122 us -> 99.5 us  [body(): packed = lax.all_gather(own, 'shard', axis=0, tiled=False)]
    all_gather x0 -> x1, blocking collectives: none -> 20.6 us  [body(): table_all = lax.all_gather(table_own, 'shard', axis=0, tiled=False)]
    ppermute x1, waiting for transfers between devices: 0.01 us -> 14.9 us  [rep_sum(): arrived = lax.ppermute(sent, 'rep', pairs)]
    pallas_call x4 -> x1, Pallas kernels: 65.4 us -> 51.1 us  [call_kernel(): pl.pallas_call(kernel, out_shape=[jax.ShapeDtypeStruct(shape, kind) for s...]
  transfers between devices with their start and end apart: 5 -> 3, of which waited for: 4 -> 3; matrix products, arithmetic and copies ran while one was open for 4% -> 2% of each run, Pallas kernels for 0% -> 0%
where the time goes in v3:
time: 372 us; the launch traced here: 371 us
  waiting for transfers between devices  249 us (67%)
  Pallas kernels  51.1 us (14%)
  local copies, waits for them, and re-layouts  24.6 us (7%)
  blocking collectives  20.6 us (6%)
  between operations  14.5 us (4%)
  other arithmetic  7.03 us (2%)
    reduce_scatter x1, waiting for transfers between devices, body(): lax.psum_scatter(weight_grads, 'shard', scatter_dimension=0, tiled=False)  135 us
    all_gather x1, waiting for transfers between devices, body(): packed = lax.all_gather(own, 'shard', axis=0, tiled=False)  99.5 us
    pallas_call x1, Pallas kernels, call_kernel(): pl.pallas_call(kernel, out_shape=[jax.ShapeDtypeStruct(shape, kind) for s...  51.1 us
    all_gather x1, blocking collectives, body(): table_all = lax.all_gather(table_own, 'shard', axis=0, tiled=False)  20.6 us
    ppermute x1, waiting for transfers between devices, rep_sum(): arrived = lax.ppermute(sent, 'rep', pairs)  14.9 us
  transfers between devices with their start and end apart: 3, of which 3 were waited for; matrix products, arithmetic and copies ran while one was open for 2% of the time, Pallas kernels for 0%

profile of v3, /device:TPU:0, one launch (start us, length us, event | category | flops | bytes accessed | tf_op | source)
XLA Modules:
  0.0 370.9 jit_solution(5693861378609302668)
XLA Ops:
  7.3 0.8 fusion.35
  10.8 1.0 slice_bitcast_fusion.2
  11.7 1.0 slice_bitcast_fusion
  12.8 0.8 constant_dynamic-update-slice_fusion.13
  13.6 0.9 bitcast_dynamic-update-slice_fusion.1
  14.5 0.8 constant_dynamic-update-slice_fusion.5
  15.3 0.9 bitcast_dynamic-update-slice_fusion
  16.3 0.9 copy-done.1
  21.9 1.0 broadcast_add_fusion.refs_5_
  22.9 99.5 %all-gather.5.cloned.1.call-done = bf16[12544,512]{1,0:T(8,128)(2,1)} async-done(((bf16[784,512]{1,0:T(8,128)(2,1)}), bf16[12544,512]{1,0:T(8,128)(2,1)}) %all-gather.5.cloned.1.call-update) | async-done | bytes 12845072 | tf_op jit(solution)/shard_map/all_gather | solution.py:431
  123.2 0.8 slice_convert_fusion
  125.5 51.1 %both_blocks.1 = (bf16[256,512]{1,0:T(8,128)(2,1)}, f32[256,512]{1,0:T(8,128)}, bf16[16,784,512]{2,1,0:T(8,128)(2,1)}, f32[2,16,512]{2,1,0:T(8,128)}, f32[2,1024,64]{2,1,0:T(8,128)}) custom-call(bf16[256,512]{1,0:T(8,128)(2,1)} %bitcast.92, bf16[256,512]{1,0:T(8,128)(2,1)} %bitcast.93, bf16[16,784,512]{2,1,0:T(8,128)(2,1)} %bitcast.100, ...), custom_call_target="tpu_custom_call" | custom-call | flops 9663676416 | bytes 20000000 | tf_op jit(solution)/shard_map/both_blocks/pallas_call | solution.py:371
  176.7 0.8 convert.20
  177.8 1.6 reshape.153
  179.4 1.6 fusion.6
  181.7 0.8 pad_dynamic-update-slice_fusion
  182.5 134.9 %reduce-scatter.2.cloned.1.call-done = bf16[1,784,512]{2,1,0:T(8,128)(2,1)} async-done(((bf16[16,784,512]{2,1,0:T(8,128)(2,1)}), bf16[1,784,512]{2,1,0:T(8,128)(2,1)}) %reduce-scatter.2.cloned.1.call-update) | async-done | bytes 802832 | tf_op jit(solution)/shard_map/reduce_scatter | solution.py:493
  317.4 1.5 collective-permute-start
  319.6 1.2 copy.80
  321.5 14.9 %collective-permute-done = bf16[784,512]{1,0:T(8,128)(2,1)S(1)} collective-permute-done((bf16[784,512]{1,0:T(8,128)(2,1)}, bf16[784,512]{1,0:T(8,128)(2,1)S(1)}, u32[]{:S(2)}, u32[]{:S(2)}) %collective-permute-start) | collective-permute-done | bytes 802848 | tf_op jit(solution)/shard_map/ppermute | solution.py:67
  337.5 0.8 slice.251
  341.0 20.6 %all-gather.2 = f32[16,2,176]{2,1,0:T(2,128)S(1)} all-gather(f32[1,2,176]{2,1,0:T(2,128)S(1)} %slice_bitcast_fusion.4), channel_id=3, replica_groups=mesh['rep'=2,'shard'=16] {'shard'}, dimensions={0}, use_global_device_ids=true | all-gather | bytes 23936 | tf_op jit(solution)/shard_map/all_gather | solution.py:497
  362.5 0.8 pad_maximum_fusion.1
  363.3 0.8 pad_maximum_fusion
  (109 shorter events, 16.7 us)
Async XLA Ops:
  7.2 12.1 %copy-start = (bf16[2,169,16]{1,2,0:T(8,128)(2,1)S(1)}, bf16[2,169,16]{1,2,0:T(8,128)(2,1)}, u32[]{:S(2)}) copy-start(bf16[2,169,16]{1,2,0:T(8,128)(2,1)} %param.26) | copy-start | bytes 32452
  7.2 10.1 %copy-start.7 = (s32[1,14,14]{2,0,1:T(1,128)S(1)}, s32[1,14,14]{2,0,1:T(1,128)}, u32[]{:S(2)}) copy-start(s32[1,14,14]{2,0,1:T(1,128)} %param.17) | copy-start | bytes 2356
  7.2 10.3 %copy-start.4 = (bf16[1,14,14,512]{3,2,1,0:T(8,128)(2,1)S(1)}, bf16[1,14,14,512]{3,2,1,0:T(8,128)(2,1)}, u32[]{:S(2)}) copy-start(bf16[1,14,14,512]{3,2,1,0:T(8,128)(2,1)} %param.15) | copy-start | bytes 602116
  7.2 10.5 %copy-start.5 = (bf16[1,14,14,512]{3,2,1,0:T(8,128)(2,1)S(1)}, bf16[1,14,14,512]{3,2,1,0:T(8,128)(2,1)}, u32[]{:S(2)}) copy-start(bf16[1,14,14,512]{3,2,1,0:T(8,128)(2,1)} %param.16) | copy-start | bytes 602116
  7.2 115.2 %all-gather.5.cloned.1.call-start = ((), (), s32[]{:S(2)}) async-start(), calls=%async_computation.2 | async-start | bytes 13647872 | tf_op jit(solution)/shard_map/all_gather | solution.py:431
  13.5 5.8 %copy-start.10 = (s32[4096]{0:T(1024)S(1)}, s32[4096]{0:T(1024)}, u32[]{:S(2)}) copy-start(s32[4096]{0:T(1024)} %constant.24.clone) | copy-start | bytes 49156
  16.3 0.9 copy-start.1
  17.2 300.2 %reduce-scatter.2.cloned.1.call-start = ((), (), s32[]{:S(2)}) async-start(), calls=%async_computation.1 | async-start | bytes 13647872 | tf_op jit(solution)/shard_map/reduce_scatter | solution.py:493
  17.5 2.8 copy-start.8
  17.5 2.8 copy-start.9
  182.5 136.4 %copy-start.6 = (bf16[256,512]{1,0:T(8,128)(2,1)S(1)}, bf16[256,512]{1,0:T(8,128)(2,1)}, u32[]{:S(2)}) copy-start(bf16[256,512]{1,0:T(8,128)(2,1)} %get-tuple-element.16) | copy-start | bytes 786436
  182.5 136.7 %copy-start.3 = (f32[256,512]{1,0:T(8,128)S(1)}, f32[256,512]{1,0:T(8,128)}, u32[]{:S(2)}) copy-start(f32[256,512]{1,0:T(8,128)} %get-tuple-element.17) | copy-start | bytes 1572868
  317.4 19.1 %copy-start.2 = (bf16[1,784,512]{2,1,0:T(8,128)(2,1)S(1)}, bf16[1,784,512]{2,1,0:T(8,128)(2,1)}, u32[]{:S(2)}) copy-start(bf16[1,784,512]{2,1,0:T(8,128)(2,1)} %reduce-scatter.2.cloned.1.call-done) | copy-start | bytes 2408452
  317.4 19.1 %collective-permute-start = (bf16[784,512]{1,0:T(8,128)(2,1)}, bf16[784,512]{1,0:T(8,128)(2,1)S(1)}, u32[]{:S(2)}, u32[]{:S(2)}) collective-permute-start(bf16[784,512]{1,0:T(8,128)(2,1)} %bitcast.83), channel_id=1, source_target_pairs={{0,16},{16,0},{1,17},{17,1},{2,18},{18,2},{3,19},{19,3},{4,20},{20... | collective-permute-start | bytes 2408456 | tf_op jit(solution)/shard_map/ppermute | solution.py:67
Sparse Core Ops, SparseCore 0:
  17.3 105.0 all-gather.4
  182.6 134.7 reduce-scatter.1
